TPU v7x, 256 devices: a whole 4x4x8 slice. The times are simulated.
256 devices in a mesh: space: 8 (over y, core), angle: 32 (over z, x).
Axes of the slice: x: 4, y: 4, z: 8, core: 2. Of those that a mesh axis runs over, the one named last changes fastest.
Arguments:
- image: float32 [32768, 128], P(('space', 'angle')), may hold values from 0 to 1
- tiles: bfloat16 [8, 3072, 128, 128], P('space', 'angle'), may hold values from -0.109375 to 0.109375
- tile_slot: int32 [8, 3072], P('space', 'angle'), may hold values from 0 to 7, as said below
- tile_block: int32 [8, 3072], P('space', 'angle'), may hold values from 0 to 31
- slot_ray: int32 [8, 256], P('space', 'angle'), may hold values from 0 to 31, as said below
- sinogram: bfloat16 [32, 32, 128, 128], P('angle', 'space'), may hold values from -4 to 4
- weights: bfloat16 [32, 32, 128, 128], P('angle', 'space'), may hold values from 0.29882812 to 3
Outputs:
- volume: float32 [32768, 128], P(('space', 'angle'))
- residual: bfloat16 [32, 32, 128, 128], P('angle', 'space')
Inputs may be any that keep to these rules, and one draw needn't show every extreme that they name: `tile_slot`: every slot of a device is fed by at least one of its tiles. `slot_ray`: the 8 entries of one device are distinct; of the ray blocks k * 4 to (k + 1) * 4 - 1 of its angle group, one device lists at most 2, and in every angle group some k is listed 2 times by every device of the group.
All inputs are finite; a program needn't handle non-finite values.
Results may differ from a plain program's by a relative error of at most 0.025.
Values may be sent and summed in bfloat16 or wider, within the bound.
No kernel may reach another device: no remote copies, remote signals or barrier semaphores. Data moves between devices by JAX's collectives and lax.ppermute only.
A program may use at most 64 MiB of HBM per device.

v0:
```python
import math

import jax
import jax.numpy as jnp
from jax import lax
from jax.sharding import PartitionSpec as P

ITERS = 2


def shards(image, tiles, tile_slot, tile_block, slot_ray, sinogram, weights):
    n_space = lax.axis_size("space")
    n_angle = lax.axis_size("angle")
    tile_mats = tiles[0]
    slot_ids = tile_slot[0]
    block_ids = tile_block[0]
    ray_ids = slot_ray[0]
    own_count = sinogram.shape[1]
    tile_edge = tile_mats.shape[1]
    slices = image.shape[1]
    share_rows = image.shape[0]
    block_count = share_rows * n_angle // tile_edge
    slot_count = ray_ids.shape[0]
    ray_count = own_count * n_space
    step_size = 0.2 * math.sqrt(block_count / (n_angle * own_count))
    observed = sinogram[0].astype(jnp.float32)
    scales = weights[0].astype(jnp.float32)
    slot_hot = (slot_ids[:, None] == jnp.arange(slot_count, dtype=jnp.int32)[None, :]).astype(
        jnp.float32
    )
    block_hot = (block_ids[:, None] == jnp.arange(block_count, dtype=jnp.int32)[None, :]).astype(
        jnp.float32
    )
    ray_hot = (ray_ids[None, :] == jnp.arange(ray_count, dtype=jnp.int32)[:, None]).astype(
        jnp.bfloat16
    )

    def ray_residual(partial_value):
        dense_terms = jnp.einsum(
            "rs,sik->rik", ray_hot, partial_value, preferred_element_type=jnp.float32
        )
        ray_sums = lax.psum_scatter(
            dense_terms.astype(jnp.bfloat16), "space", scatter_dimension=0, tiled=True
        ).astype(jnp.float32)
        residual = (scales * (ray_sums - observed)).astype(jnp.bfloat16)
        whole_rays = lax.all_gather(residual, "space", axis=0, tiled=True)
        slot_res = jnp.einsum(
            "rs,rik->sik", ray_hot, whole_rays, preferred_element_type=jnp.float32
        ).astype(jnp.bfloat16)
        return (residual, slot_res)

    current = image
    pixels = lax.all_gather(current.astype(jnp.bfloat16), "angle", axis=0, tiled=True)
    for iteration in range(ITERS):
        blocks = pixels.reshape(block_count, tile_edge, slices)
        picked = jnp.take(blocks, block_ids, axis=0)
        products = jnp.einsum("tij,tjk->tik", tile_mats, picked, preferred_element_type=jnp.float32)
        gradient_partial_value = jnp.einsum(
            "ts,tik->sik", slot_hot, products, precision=lax.Precision.HIGHEST
        ).astype(jnp.bfloat16)
        gradient_residual, gradient_slot_res = ray_residual(gradient_partial_value)
        tile_res = jnp.take(gradient_slot_res, slot_ids, axis=0)
        back_terms = jnp.einsum(
            "tji,tjk->tik", tile_mats, tile_res, preferred_element_type=jnp.float32
        )
        block_terms = jnp.einsum(
            "tb,tik->bik", block_hot, back_terms, precision=lax.Precision.HIGHEST
        )
        grad_part = block_terms.reshape(block_count * tile_edge, slices)
        residual = gradient_residual
        gradient = lax.psum_scatter(
            grad_part.astype(jnp.bfloat16), "angle", scatter_dimension=0, tiled=True
        ).astype(jnp.float32)
        current = jnp.maximum(current - step_size * gradient, 0.0)
        if iteration + 1 < ITERS:
            pixels = lax.all_gather(current.astype(jnp.bfloat16), "angle", axis=0, tiled=True)
    return (current, residual[None])


def solution(mesh):
    placed = (
        P(("space", "angle"), None),
        P("space", "angle", None, None),
        P("space", "angle"),
        P("space", "angle"),
        P("space", "angle"),
        P("angle", "space", None, None),
        P("angle", "space", None, None),
    )
    return jax.shard_map(
        shards,
        mesh=mesh,
        in_specs=placed,
        out_specs=(P(("space", "angle"), None), P("angle", "space", None, None)),
        check_vma=False,
    )
```

profile of v0, /device:TPU:8, one launch (start us, length us, event | category | flops | bytes accessed | tf_op | source)
XLA Modules:
  0.0 827.4 jit_solution(5247489536463539266)
XLA Ops:
  7.2 1.6 convert_element_type.71
  10.2 80.1 %all-gather.5.cloned.1.call-done = bf16[4096,128]{1,0:T(8,128)(2,1)} async-done(((bf16[128,128]{1,0:T(8,128)(2,1)}), bf16[4096,128]{1,0:T(8,128)(2,1)}) %all-gather.5.cloned.1.call-update) | async-done | bytes 1048592 | tf_op jit(solution)/shard_map/all_gather | solution.py:53
  90.4 4.0 gather_fusion
  94.3 7.0 fusion.16
  101.4 6.7 copy.30
  108.1 4.9 convolution_convert_fusion.5
  115.1 29.5 %reduce-scatter.5.cloned.1.call-done = bf16[4,128,128]{2,1,0:T(8,128)(2,1)} async-done(((bf16[32,128,128]{2,1,0:T(8,128)(2,1)}), bf16[4,128,128]{2,1,0:T(8,128)(2,1)}) %reduce-scatter.5.cloned.1.call-update) | async-done | bytes 131088 | tf_op jit(solution)/shard_map/reduce_scatter | solution.py:42
  144.5 1.6 fusion.42
  146.5 26.6 %all-gather.7.cloned.1.call-done = bf16[32,128,128]{2,1,0:T(8,128)(2,1)} async-done(((bf16[4,128,128]{2,1,0:T(8,128)(2,1)}), bf16[32,128,128]{2,1,0:T(8,128)(2,1)}) %all-gather.7.cloned.1.call-update) | async-done | bytes 1048592 | tf_op jit(solution)/shard_map/all_gather | solution.py:46
  173.1 1.9 convolution_convert_fusion.7
  175.0 2.8 gather_fusion.1
  177.8 5.9 fusion.21
  183.6 6.7 copy.35
  190.4 5.2 convolution_convert_fusion.2
  195.6 1.4 copy.36
  197.1 219.0 %reduce-scatter.7.cloned.1.call-done = bf16[128,128]{1,0:T(8,128)(2,1)} async-done(((bf16[4096,128]{1,0:T(8,128)(2,1)}), bf16[128,128]{1,0:T(8,128)(2,1)}) %reduce-scatter.7.cloned.1.call-update) | async-done | bytes 32784 | tf_op jit(solution)/shard_map/reduce_scatter | solution.py:71
  417.5 76.1 %all-gather.9.cloned.1.call-done = bf16[4096,128]{1,0:T(8,128)(2,1)} async-done(((bf16[128,128]{1,0:T(8,128)(2,1)}), bf16[4096,128]{1,0:T(8,128)(2,1)}) %all-gather.9.cloned.1.call-update) | async-done | bytes 1048592 | tf_op jit(solution)/shard_map/all_gather | solution.py:76
  493.6 4.0 gather_fusion.2
  497.6 7.0 fusion.26
  504.6 6.7 copy.38
  511.3 4.9 convolution_convert_fusion.4
  516.8 1.4 copy.39
  518.5 29.2 %reduce-scatter.9.cloned.1.call-done = bf16[4,128,128]{2,1,0:T(8,128)(2,1)} async-done(((bf16[32,128,128]{2,1,0:T(8,128)(2,1)}), bf16[4,128,128]{2,1,0:T(8,128)(2,1)}) %reduce-scatter.9.cloned.1.call-update) | async-done | bytes 131088 | tf_op jit(solution)/shard_map/reduce_scatter | solution.py:42
  547.7 1.6 fusion.43
  549.4 26.8 %all-gather.11.cloned.1.call-done = bf16[32,128,128]{2,1,0:T(8,128)(2,1)} async-done(((bf16[4,128,128]{2,1,0:T(8,128)(2,1)}), bf16[32,128,128]{2,1,0:T(8,128)(2,1)}) %all-gather.11.cloned.1.call-update) | async-done | bytes 1048592 | tf_op jit(solution)/shard_map/all_gather | solution.py:46
  576.2 1.9 convolution_convert_fusion.6
  578.2 2.8 gather_fusion.3
  580.9 5.9 fusion.31
  586.8 6.7 copy.43
  593.5 5.2 convolution_convert_fusion
  600.2 219.0 %reduce-scatter.11.cloned.1.call-done = bf16[128,128]{1,0:T(8,128)(2,1)} async-done(((bf16[4096,128]{1,0:T(8,128)(2,1)}), bf16[128,128]{1,0:T(8,128)(2,1)}) %reduce-scatter.11.cloned.1.call-update) | async-done | bytes 32784 | tf_op jit(solution)/shard_map/reduce_scatter | solution.py:71
  819.2 1.4 subtract_maximum_fusion
  (49 shorter events, 7.6 us)
Async XLA Ops:
  7.2 87.2 %copy-start = (bf16[1,96,128,128]{3,2,1,0:T(8,128)(2,1)S(1)}, bf16[1,96,128,128]{3,2,1,0:T(8,128)(2,1)}, u32[]{:S(2)}) copy-start(bf16[1,96,128,128]{3,2,1,0:T(8,128)(2,1)} %param.12) | copy-start | bytes 9437188
  7.2 83.2 %all-gather.5.cloned.1.call-start = ((), (), s32[]{:S(2)}) async-start(), calls=%async_computation.4 | async-start | bytes 1081344 | tf_op jit(solution)/shard_map/all_gather | solution.py:53
  8.9 135.7 %reduce-scatter.5.cloned.1.call-start = ((), (), s32[]{:S(2)}) async-start(), calls=%async_computation.5 | async-start | bytes 1179648 | tf_op jit(solution)/shard_map/reduce_scatter | solution.py:42
  101.4 6.7 copy-start.8
  108.1 4.9 copy-start.7
  113.0 31.5 %copy-start.2 = (bf16[1,4,128,128]{3,2,1,0:T(8,128)(2,1)S(1)}, bf16[1,4,128,128]{3,2,1,0:T(8,128)(2,1)}, u32[]{:S(2)}) copy-start(bf16[1,4,128,128]{3,2,1,0:T(8,128)(2,1)} %param.16) | copy-start | bytes 393220
  113.0 31.5 %copy-start.4 = (bf16[1,4,128,128]{3,2,1,0:T(8,128)(2,1)S(1)}, bf16[1,4,128,128]{3,2,1,0:T(8,128)(2,1)}, u32[]{:S(2)}) copy-start(bf16[1,4,128,128]{3,2,1,0:T(8,128)(2,1)} %param.17) | copy-start | bytes 393220
  115.0 58.0 %all-gather.7.cloned.1.call-start = ((), (), s32[]{:S(2)}) async-start(), calls=%async_computation.6 | async-start | bytes 1179648 | tf_op jit(solution)/shard_map/all_gather | solution.py:46
  146.2 269.9 %reduce-scatter.7.cloned.1.call-start = ((), (), s32[]{:S(2)}) async-start(), calls=%async_computation.7 | async-start | bytes 1081344 | tf_op jit(solution)/shard_map/reduce_scatter | solution.py:71
  183.6 6.7 copy-start.9
  195.6 220.5 %copy-start.1 = (f32[128,128]{1,0:T(8,128)S(1)}, f32[128,128]{1,0:T(8,128)}, u32[]{:S(2)}) copy-start(f32[128,128]{1,0:T(8,128)} %param.11) | copy-start | bytes 196612
  197.0 296.6 %all-gather.9.cloned.1.call-start = ((), (), s32[]{:S(2)}) async-start(), calls=%async_computation.8 | async-start | bytes 1081344 | tf_op jit(solution)/shard_map/all_gather | solution.py:76
  417.5 130.3 %reduce-scatter.9.cloned.1.call-start = ((), (), s32[]{:S(2)}) async-start(), calls=%async_computation.9 | async-start | bytes 1179648 | tf_op jit(solution)/shard_map/reduce_scatter | solution.py:42
  516.3 31.5 %copy-start.3 = (bf16[1,4,128,128]{3,2,1,0:T(8,128)(2,1)S(1)}, bf16[1,4,128,128]{3,2,1,0:T(8,128)(2,1)}, u32[]{:S(2)}) copy-start(bf16[1,4,128,128]{3,2,1,0:T(8,128)(2,1)} %param.16) | copy-start | bytes 393220
  516.3 31.5 %copy-start.5 = (bf16[1,4,128,128]{3,2,1,0:T(8,128)(2,1)S(1)}, bf16[1,4,128,128]{3,2,1,0:T(8,128)(2,1)}, u32[]{:S(2)}) copy-start(bf16[1,4,128,128]{3,2,1,0:T(8,128)(2,1)} %param.17) | copy-start | bytes 393220
  518.3 58.0 %all-gather.11.cloned.1.call-start = ((), (), s32[]{:S(2)}) async-start(), calls=%async_computation.10 | async-start | bytes 1179648 | tf_op jit(solution)/shard_map/all_gather | solution.py:46
  549.4 269.8 %reduce-scatter.11.cloned.1.call-start = ((), (), s32[]{:S(2)}) async-start(), calls=%async_computation.11 | async-start | bytes 1081344 | tf_op jit(solution)/shard_map/reduce_scatter | solution.py:71
  598.8 220.4 %copy-start.6 = (bf16[128,128]{1,0:T(8,128)(2,1)S(1)}, bf16[128,128]{1,0:T(8,128)(2,1)}, u32[]{:S(2)}) copy-start(bf16[128,128]{1,0:T(8,128)(2,1)} %reduce-scatter.7.cloned.1.call-done) | copy-start | bytes 98308
Sparse Core Ops, SparseCore 0:
  11.1 79.1 all-gather.4
  115.2 29.3 reduce-scatter.4
  147.0 26.0 all-gather.6
  197.2 218.8 reduce-scatter.6
  419.1 74.5 all-gather.8
  518.4 29.3 reduce-scatter.8
  550.2 26.0 all-gather.10
  600.3 218.7 reduce-scatter.10
where the time goes:
time: 828 us; the launch traced here: 827 us
  waiting for transfers between devices  706 us (85%)
  matrix products  50.8 us (6%)
  local copies, waits for them, and re-layouts  46.2 us (6%)
  between operations  14.3 us (2%)
  other arithmetic  8.98 us (1%)
    reduce_scatter x2, waiting for transfers between devices, shards(): lax.psum_scatter(grad_part.astype(jnp.bfloat16), 'angle', scatter_dimensi...  438 us
    all_gather x2, waiting for transfers between devices, shards(): lax.all_gather(current.astype(jnp.bfloat16), 'angle', axis=0, tiled=True)  156 us
    reduce_scatter x2, waiting for transfers between devices, ray_residual(): lax.psum_scatter(dense_terms.astype(jnp.bfloat16), 'space', scatter_dimen...  58.7 us
    all_gather x2, waiting for transfers between devices, ray_residual(): whole_rays = lax.all_gather(residual, 'space', axis=0, tiled=True)  53.4 us
  transfers between devices with their start and end apart: 8, of which 8 were waited for; matrix products, arithmetic and copies ran while one was open for 0% of the time, Pallas kernels for 0%

commit v1 on v0

v1 whole, which is shorter than its diff:
```python
import functools
import math

import jax
import jax.numpy as jnp
from jax import lax
from jax.experimental import pallas as pl
from jax.experimental.pallas import tpu as pltpu
from jax.sharding import PartitionSpec as P

ITERS = 2
CAP = 2
NX = 4
META = 16
UNROLL = 8

SMEM = pl.BlockSpec(memory_space=pltpu.SMEM)
VMEM = pl.BlockSpec(memory_space=pltpu.VMEM)


def params(mib):
    return pltpu.CompilerParams(vmem_limit_bytes=mib << 20)


def place_slots(ray_ref, pos_ref, idx_ref, own):
    slots = ray_ref.shape[0]
    for seat in range(idx_ref.shape[0]):
        idx_ref[seat] = -1
    rays = [ray_ref[j] for j in range(slots)]
    owners = [r // own for r in rays]
    for j in range(slots):
        rank = jnp.int32(0)
        for i in range(j):
            rank += (owners[i] == owners[j]).astype(jnp.int32)
        seat = owners[j] * CAP + jnp.minimum(rank, CAP - 1)
        pos_ref[j] = seat
        idx_ref[seat] = rays[j] - owners[j] * own


def block_seat(b, nz):
    return (b % NX) * nz + b // NX


def forward_kernel(own, slot_ref, block_ref, ray_ref, tiles_ref, pix_ref, out_ref, acc, pos, idx):
    nz = pix_ref.shape[0] // NX
    tiles, edge, _ = tiles_ref.shape
    place_slots(ray_ref, pos, idx, own)
    acc[...] = jnp.zeros_like(acc)
    out_ref[...] = jnp.zeros_like(out_ref)

    def step(i, carry):
        for u in range(UNROLL):
            t = i * UNROLL + u
            j = slot_ref[t]
            p = block_seat(block_ref[t], nz)
            acc[j] += jnp.dot(tiles_ref[t], pix_ref[p], preferred_element_type=jnp.float32)
        return carry

    lax.fori_loop(0, tiles // UNROLL, step, 0)
    for j in range(acc.shape[0]):
        seat = pos[j]
        out_ref[seat // CAP, pl.ds(pl.multiple_of((seat % CAP) * edge, edge), edge), :] = acc[j].astype(
            jnp.bfloat16
        )
    if out_ref.shape[1] > CAP * edge:
        row = lax.broadcasted_iota(jnp.int32, (META, out_ref.shape[2]), 0)
        for k in range(out_ref.shape[0]):
            value = jnp.where(row < META // CAP, idx[k * CAP], idx[k * CAP + 1])
            out_ref[k, pl.ds(CAP * edge, META), :] = value.astype(jnp.float32).astype(jnp.bfloat16)


def owner_kernel(recv_ref, meta_ref, obs_ref, scale_ref, res_ref, back_ref):
    spaces = recv_ref.shape[0]
    own, edge, slices = obs_ref.shape
    step = 16
    seats = [(s, r) for s in range(spaces) for r in range(CAP)]
    marks = {}
    for s in range(spaces):
        value = meta_ref[s].astype(jnp.float32)
        for r in range(CAP):
            marks[s, r] = value[r * (META // CAP) : r * (META // CAP) + 1, :]
    for c in range(edge // step):
        sums = [jnp.zeros((step, slices), jnp.float32) for _ in range(own)]
        for s, r in seats:
            data = recv_ref[s, r * edge + c * step : r * edge + (c + 1) * step, :].astype(jnp.float32)
            mark = jnp.broadcast_to(marks[s, r], (step, slices))
            for o in range(own):
                sums[o] += jnp.where(mark == float(o), data, 0.0)
        rows = slice(c * step, (c + 1) * step)
        for o in range(own):
            obs = obs_ref[o, rows, :].astype(jnp.float32)
            scale = scale_ref[o, rows, :].astype(jnp.float32)
            res_ref[o, rows, :] = (scale * (sums[o] - obs)).astype(jnp.bfloat16)
    flipped = [res_ref[o].astype(jnp.float32).T for o in range(own)]
    for s, r in seats:
        mark = jnp.broadcast_to(marks[s, r], (edge, slices))
        value = flipped[own - 1]
        for o in range(own - 1):
            value = jnp.where(mark == float(o), flipped[o], value)
        back_ref[s, r * edge : (r + 1) * edge, :] = value.astype(jnp.bfloat16)


def backward_kernel(own, slot_ref, block_ref, ray_ref, tiles_ref, res_ref, out_ref, acc, pos, idx):
    nz = out_ref.shape[0] // NX
    tiles = tiles_ref.shape[0]
    place_slots(ray_ref, pos, idx, own)
    acc[...] = jnp.zeros_like(acc)

    def step(i, carry):
        for u in range(UNROLL):
            t = i * UNROLL + u
            seat = pos[slot_ref[t]]
            p = block_seat(block_ref[t], nz)
            acc[p] += jnp.dot(res_ref[seat], tiles_ref[t], preferred_element_type=jnp.float32)
        return carry

    lax.fori_loop(0, tiles // UNROLL, step, 0)
    out_ref[...] = acc[...].astype(jnp.bfloat16)


def update_kernel(step_size, grad_ref, cur_ref, new_ref, *copies):
    total = grad_ref[0].astype(jnp.float32)
    for k in range(1, grad_ref.shape[0]):
        total += grad_ref[k].astype(jnp.float32)
    new = jnp.maximum(cur_ref[...] - step_size * total.T, 0.0)
    new_ref[...] = new
    for copy in copies:
        value = new.astype(jnp.bfloat16)
        for k in range(copy.shape[0]):
            copy[k] = value


def shards(image, tiles, tile_slot, tile_block, slot_ray, sinogram, weights):
    n_space = lax.axis_size("space")
    n_angle = lax.axis_size("angle")
    nz = n_angle // NX
    x_groups = [[z * NX + x for x in range(NX)] for z in range(nz)]
    z_groups = [[z * NX + x for z in range(nz)] for x in range(NX)]
    tile_mats = tiles[0]
    own = sinogram.shape[1]
    edge = tile_mats.shape[1]
    slices = image.shape[1]
    blocks = image.shape[0] * n_angle // edge
    slots = slot_ray.shape[1]
    step_size = 0.2 * math.sqrt(blocks / (n_angle * own))
    obs, scale = sinogram[0], weights[0]
    lists = (tile_slot[0], tile_block[0], slot_ray[0])
    bf16, f32 = jnp.bfloat16, jnp.float32
    seats = pltpu.SMEM((slots,), jnp.int32), pltpu.SMEM((n_space * CAP,), jnp.int32)

    def to_all(x, axis, groups=None):
        return lax.all_to_all(x, axis, 0, 0, axis_index_groups=groups, tiled=True)

    def gather(copies):
        column = to_all(copies, "angle", z_groups)
        wide = jnp.broadcast_to(column[None], (NX, nz, edge, slices)).reshape(blocks, edge, slices)
        return to_all(wide, "angle", x_groups)

    current = image
    pixels = gather(jnp.broadcast_to(image.astype(bf16)[None], (nz, edge, slices)))
    meta = None
    for iteration in range(ITERS):
        rows = CAP * edge + (META if iteration == 0 else 0)
        sent = pl.pallas_call(
            functools.partial(forward_kernel, own),
            out_shape=jax.ShapeDtypeStruct((n_space, rows, slices), bf16),
            in_specs=[SMEM] * 3 + [VMEM] * 2,
            out_specs=VMEM,
            scratch_shapes=[pltpu.VMEM((slots, edge, slices), f32), *seats],
            compiler_params=params(12),
            name="forward",
        )(*lists, tile_mats, pixels)
        recv = to_all(sent, "space")
        if iteration == 0:
            meta = recv[:, CAP * edge :, :]
        residual, back = pl.pallas_call(
            owner_kernel,
            out_shape=(
                jax.ShapeDtypeStruct((own, edge, slices), bf16),
                jax.ShapeDtypeStruct((n_space, CAP * edge, slices), bf16),
            ),
            in_specs=[VMEM] * 4,
            out_specs=(VMEM, VMEM),
            compiler_params=params(12),
            name="owner",
        )(recv, meta, obs, scale)
        slot_res = to_all(back, "space").reshape(n_space * CAP, slices, edge)
        grad_part = pl.pallas_call(
            functools.partial(backward_kernel, own),
            out_shape=jax.ShapeDtypeStruct((blocks, slices, edge), bf16),
            in_specs=[SMEM] * 3 + [VMEM] * 2,
            out_specs=VMEM,
            scratch_shapes=[pltpu.VMEM((blocks, slices, edge), f32), *seats],
            compiler_params=params(16),
            name="backward",
        )(*lists, tile_mats, slot_res)
        across = to_all(grad_part, "angle", x_groups).reshape(NX, nz, slices, edge)
        column = jnp.sum(across.astype(f32), axis=0).astype(bf16)
        terms = to_all(column, "angle", z_groups)
        more = iteration + 1 < ITERS
        shapes = [jax.ShapeDtypeStruct((edge, slices), f32)]
        if more:
            shapes.append(jax.ShapeDtypeStruct((nz, edge, slices), bf16))
        current, *copies = pl.pallas_call(
            functools.partial(update_kernel, step_size),
            out_shape=tuple(shapes),
            in_specs=[VMEM] * 2,
            out_specs=(VMEM,) * len(shapes),
            compiler_params=params(8),
            name="update",
        )(terms, current)
        if more:
            pixels = gather(copies[0])
    return (current, residual[None])


def solution(mesh):
    placed = (
        P(("space", "angle"), None),
        P("space", "angle", None, None),
        P("space", "angle"),
        P("space", "angle"),
        P("space", "angle"),
        P("angle", "space", None, None),
        P("angle", "space", None, None),
    )
    return jax.shard_map(
        shards,
        mesh=mesh,
        in_specs=placed,
        out_specs=(P(("space", "angle"), None), P("angle", "space", None, None)),
        check_vma=False,
    )
```

time: 828 us -> 204 us (0.25)
  waiting for transfers between devices: 706 us -> 0 us
  blocking collectives: 0 us -> 181 us
  matrix products: 50.8 us -> 0 us
  local copies, waits for them, and re-layouts: 46.2 us -> 1.16 us
  Pallas kernels: 0 us -> 17.1 us
  between operations: 14.3 us -> 0.78 us
    reduce_scatter x4 -> x0, waiting for transfers between devices: 497 us -> none  [the longest x2 438 us: shards(): lax.psum_scatter(grad_part.astype(jnp.bfloat16), 'angle', scatter_dimensi...]
    all_gather x4 -> x0, waiting for transfers between devices: 210 us -> none  [the longest x2 156 us: shards(): lax.all_gather(current.astype(jnp.bfloat16), 'angle', axis=0, tiled=True)]
    all_to_all x0 -> x12, blocking collectives: none -> 181 us  [to_all(): return lax.all_to_all(x, axis, 0, 0, axis_index_groups=groups, tiled=True)]
    dot_general x12 -> x0, matrix products: 50.8 us -> none  [the longest x2 14 us: shards(): jnp.einsum('tij,tjk->tik', tile_mats, picked, preferred_element_type=jnp....]
    dot_general x4 -> x0, local copies, waits for them, and re-layouts: 26.9 us -> none  [the longest x2 13.5 us: shards(): jnp.einsum('tij,tjk->tik', tile_mats, picked, preferred_element_type=jnp....]
    pallas_call x0 -> x8, Pallas kernels: none -> 17.1 us  [the longest x2 7.08 us: shards(): pl.pallas_call(functools.partial(forward_kernel, own), out_shape=jax.Shap...]
    gather x4 -> x0, local copies, waits for them, and re-layouts: 13.5 us -> none  [the longest x2 7.98 us: shards(): picked = jnp.take(blocks, block_ids, axis=0)]
  transfers between devices with their start and end apart: 8 -> 0, of which waited for: 8 -> 0; matrix products, arithmetic and copies ran while one was open for 0% -> 0% of each run, Pallas kernels for 0% -> 0%
where the time goes in v1:
time: 204 us; the launch traced here: 203 us
  blocking collectives  181 us (89%)
  Pallas kernels  17.1 us (8%)
  other arithmetic  3.37 us (2%)
    all_to_all x12, blocking collectives, to_all(): return lax.all_to_all(x, axis, 0, 0, axis_index_groups=groups, tiled=True)  181 us
    pallas_call x2, Pallas kernels, shards(): pl.pallas_call(functools.partial(forward_kernel, own), out_shape=jax.Shap...  7.08 us
    pallas_call x2, Pallas kernels, shards(): pl.pallas_call(functools.partial(backward_kernel, own), out_shape=jax.Sha...  7.06 us

profile of v1, /device:TPU:8, one launch (start us, length us, event | category | flops | bytes accessed | tf_op | source)
XLA Modules:
  0.0 203.1 jit_solution(10318661802283198538)
XLA Ops:
  0.6 0.0 copy-start.8
  0.6 0.0 copy-start.7
  0.7 0.0 copy-start.6
  0.7 1.0 convert_element_type.2
  1.7 20.1 %all_to_all.60 = bf16[8,128,128]{2,1,0:T(8,128)(2,1)S(1)} all-to-all(bf16[8,128,128]{2,1,0:T(8,128)(2,1)S(1)} %broadcast_in_dim.8), channel_id=1, replica_groups={{0,4,8,12,16,20,24,28},{1,5,9,13,17,21,25,29},{2,6,10,14,18,22,26,30},{..., dimensions={0} | all-to-all | bytes 524288 | tf_op jit(solution)/shard_map/all_to_all | solution.py:152
  21.8 0.2 broadcast_in_dim.9
  22.1 17.5 %all_to_all.61.pix_ref = bf16[32,128,128]{2,1,0:T(8,128)(2,1)S(1)} all-to-all(bf16[32,128,128]{2,1,0:T(8,128)(2,1)S(1)} %bitcast.35), channel_id=1, replica_groups={{0,1,2,3},{4,5,6,7},{8,9,10,11},{12,13,14,15},{16,17,18,19},{20,21,22,2..., dimensions={0} | all-to-all | bytes 2097152 | tf_op jit(solution)/shard_map/all_to_all | solution.py:152
  39.6 3.5 %forward.2 = bf16[8,272,128]{2,1,0:T(8,128)(2,1)S(1)} custom-call(s32[96]{0:T(128)S(1)} %bitcast.23, s32[96]{0:T(128)S(1)} %bitcast.27, s32[8]{0:T(128)S(1)} %bitcast.31, bf16[96,128,128]{2,1,0:T(8,128)(2,1)S(1)} %bitcast.13, bf16[32,128,128]{2,1,0:T(8,128)(2,1)S(1)} %all_to_all.61.pix_ref), custom_call_target="tpu_custom_call" | custom-call | tf_op jit(solution)/shard_map/forward/pallas_call | solution.py:164
  43.2 14.0 %all_to_all.62.recv_ref = bf16[8,272,128]{2,1,0:T(8,128)(2,1)S(1)} all-to-all(bf16[8,272,128]{2,1,0:T(8,128)(2,1)S(1)} %forward.2), channel_id=1, replica_groups=mesh['space'=8,'angle'=32] {'space'}, dimensions={0} | all-to-all | bytes 1114112 | tf_op jit(solution)/shard_map/all_to_all | solution.py:152
  57.2 1.1 owner.2
  58.3 12.8 %all_to_all.63 = bf16[8,256,128]{2,1,0:T(8,128)(2,1)S(1)} all-to-all(bf16[8,256,128]{2,1,0:T(8,128)(2,1)S(1)} %get-tuple-element.7), channel_id=1, replica_groups=mesh['space'=8,'angle'=32] {'space'}, dimensions={0} | all-to-all | bytes 1048576 | tf_op jit(solution)/shard_map/all_to_all | solution.py:152
  71.0 3.5 %backward.2 = bf16[32,128,128]{2,1,0:T(8,128)(2,1)S(1)} custom-call(s32[96]{0:T(128)S(1)} %bitcast.24, s32[96]{0:T(128)S(1)} %bitcast.28, s32[8]{0:T(128)S(1)} %bitcast.32, bf16[96,128,128]{2,1,0:T(8,128)(2,1)S(1)} %bitcast.14, bf16[16,128,128]{2,1,0:T(8,128)(2,1)S(1)} %bitcast.17), custom_call_target="tpu_custom_call" | custom-call | tf_op jit(solution)/shard_map/backward/pallas_call | solution.py:188
  74.6 0.0 copy-start.3
  74.6 18.3 %all_to_all.64 = bf16[32,128,128]{2,1,0:T(8,128)(2,1)} all-to-all(bf16[32,128,128]{2,1,0:T(8,128)(2,1)S(1)} %backward.2), channel_id=1, replica_groups={{0,1,2,3},{4,5,6,7},{8,9,10,11},{12,13,14,15},{16,17,18,19},{20,21,22,2..., dimensions={0} | all-to-all | bytes 2097152 | tf_op jit(solution)/shard_map/all_to_all | solution.py:152
  92.8 2.2 %reduce_sum.24 = bf16[8,128,128]{2,1,0:T(8,128)(2,1)} reduce(bf16[4,8,128,128]{3,2,1,0:T(8,128)(2,1)} %bitcast.38, bf16[]{:T(256)} %constant.3.clone.1), dimensions={0}, to_apply=%region_0.0 | reduce | flops 393216 | bytes 1310722 | tf_op jit(solution)/shard_map/reduce_sum | solution.py:198
  95.0 14.2 %all_to_all.65.grad_ref = bf16[8,128,128]{2,1,0:T(8,128)(2,1)S(1)} all-to-all(bf16[8,128,128]{2,1,0:T(8,128)(2,1)} %reduce_sum.24), channel_id=1, replica_groups={{0,4,8,12,16,20,24,28},{1,5,9,13,17,21,25,29},{2,6,10,14,18,22,26,30},{..., dimensions={0} | all-to-all | bytes 524288 | tf_op jit(solution)/shard_map/all_to_all | solution.py:152
  109.3 0.1 update.2
  109.4 0.0 copy-start.4
  109.4 0.6 copy-done.4
  110.0 12.9 %all_to_all.66 = bf16[8,128,128]{2,1,0:T(8,128)(2,1)S(1)} all-to-all(bf16[8,128,128]{2,1,0:T(8,128)(2,1)S(1)} %get-tuple-element.8), channel_id=1, replica_groups={{0,4,8,12,16,20,24,28},{1,5,9,13,17,21,25,29},{2,6,10,14,18,22,26,30},{..., dimensions={0} | all-to-all | bytes 524288 | tf_op jit(solution)/shard_map/all_to_all | solution.py:152
  122.9 0.2 broadcast_in_dim.10
  123.1 14.5 %all_to_all.67.pix_ref = bf16[32,128,128]{2,1,0:T(8,128)(2,1)S(1)} all-to-all(bf16[32,128,128]{2,1,0:T(8,128)(2,1)S(1)} %bitcast.36), channel_id=1, replica_groups={{0,1,2,3},{4,5,6,7},{8,9,10,11},{12,13,14,15},{16,17,18,19},{20,21,22,2..., dimensions={0} | all-to-all | bytes 2097152 | tf_op jit(solution)/shard_map/all_to_all | solution.py:152
  137.7 3.5 %forward.3 = bf16[8,256,128]{2,1,0:T(8,128)(2,1)S(1)} custom-call(s32[96]{0:T(128)S(1)} %bitcast.25, s32[96]{0:T(128)S(1)} %bitcast.29, s32[8]{0:T(128)S(1)} %bitcast.33, bf16[96,128,128]{2,1,0:T(8,128)(2,1)S(1)} %bitcast.15, bf16[32,128,128]{2,1,0:T(8,128)(2,1)S(1)} %all_to_all.67.pix_ref), custom_call_target="tpu_custom_call" | custom-call | tf_op jit(solution)/shard_map/forward/pallas_call | solution.py:164
  141.2 12.7 %all_to_all.68.recv_ref = bf16[8,256,128]{2,1,0:T(8,128)(2,1)S(1)} all-to-all(bf16[8,256,128]{2,1,0:T(8,128)(2,1)S(1)} %forward.3), channel_id=1, replica_groups=mesh['space'=8,'angle'=32] {'space'}, dimensions={0} | all-to-all | bytes 1048576 | tf_op jit(solution)/shard_map/all_to_all | solution.py:152
  153.9 1.1 owner.3
  155.0 12.8 %all_to_all.69 = bf16[8,256,128]{2,1,0:T(8,128)(2,1)S(1)} all-to-all(bf16[8,256,128]{2,1,0:T(8,128)(2,1)S(1)} %get-tuple-element.9), channel_id=1, replica_groups=mesh['space'=8,'angle'=32] {'space'}, dimensions={0} | all-to-all | bytes 1048576 | tf_op jit(solution)/shard_map/all_to_all | solution.py:152
  167.7 3.5 %backward.3 = bf16[32,128,128]{2,1,0:T(8,128)(2,1)S(1)} custom-call(s32[96]{0:T(128)S(1)} %bitcast.26, s32[96]{0:T(128)S(1)} %bitcast.30, s32[8]{0:T(128)S(1)} %bitcast.34, bf16[96,128,128]{2,1,0:T(8,128)(2,1)S(1)} %bitcast.16, bf16[16,128,128]{2,1,0:T(8,128)(2,1)S(1)} %bitcast.18), custom_call_target="tpu_custom_call" | custom-call | tf_op jit(solution)/shard_map/backward/pallas_call | solution.py:188
  171.3 0.0 copy-start.5
  171.3 17.6 %all_to_all.70 = bf16[32,128,128]{2,1,0:T(8,128)(2,1)S(1)} all-to-all(bf16[32,128,128]{2,1,0:T(8,128)(2,1)S(1)} %backward.3), channel_id=1, replica_groups={{0,1,2,3},{4,5,6,7},{8,9,10,11},{12,13,14,15},{16,17,18,19},{20,21,22,2..., dimensions={0} | all-to-all | bytes 2097152 | tf_op jit(solution)/shard_map/all_to_all | solution.py:152
  188.8 0.2 reduce_sum.25
  189.0 13.3 %all_to_all.71.grad_ref = bf16[8,128,128]{2,1,0:T(8,128)(2,1)S(1)} all-to-all(bf16[8,128,128]{2,1,0:T(8,128)(2,1)S(1)} %reduce_sum.25), channel_id=1, replica_groups={{0,4,8,12,16,20,24,28},{1,5,9,13,17,21,25,29},{2,6,10,14,18,22,26,30},{..., dimensions={0} | all-to-all | bytes 524288 | tf_op jit(solution)/shard_map/all_to_all | solution.py:152
  202.4 0.7 update.3
  (13 shorter events, 0.1 us)
Async XLA Ops:
  0.6 39.0 %copy-start.8 = (s32[1,8]{1,0:T(1,128)S(1)}, s32[1,8]{1,0:T(1,128)}, u32[]{:S(2)}) copy-start(s32[1,8]{1,0:T(1,128)} %param.11) | copy-start | bytes 100
  0.6 39.0 %copy-start.7 = (s32[1,96]{1,0:T(1,128)S(1)}, s32[1,96]{1,0:T(1,128)}, u32[]{:S(2)}) copy-start(s32[1,96]{1,0:T(1,128)} %param.10) | copy-start | bytes 1156
  0.7 39.0 %copy-start.6 = (s32[1,96]{1,0:T(1,128)S(1)}, s32[1,96]{1,0:T(1,128)}, u32[]{:S(2)}) copy-start(s32[1,96]{1,0:T(1,128)} %param.9) | copy-start | bytes 1156
  0.7 39.0 %copy-start = (bf16[1,96,128,128]{3,2,1,0:T(8,128)(2,1)S(1)}, bf16[1,96,128,128]{3,2,1,0:T(8,128)(2,1)}, u32[]{:S(2)}) copy-start(bf16[1,96,128,128]{3,2,1,0:T(8,128)(2,1)} %param.8) | copy-start | bytes 9437188
  39.6 17.6 %copy-start.1 = (bf16[1,4,128,128]{3,2,1,0:T(8,128)(2,1)S(1)}, bf16[1,4,128,128]{3,2,1,0:T(8,128)(2,1)}, u32[]{:S(2)}) copy-start(bf16[1,4,128,128]{3,2,1,0:T(8,128)(2,1)} %param.12) | copy-start | bytes 393220
  39.6 17.6 %copy-start.2 = (bf16[1,4,128,128]{3,2,1,0:T(8,128)(2,1)S(1)}, bf16[1,4,128,128]{3,2,1,0:T(8,128)(2,1)}, u32[]{:S(2)}) copy-start(bf16[1,4,128,128]{3,2,1,0:T(8,128)(2,1)} %param.13) | copy-start | bytes 393220
  74.6 34.7 %copy-start.3 = (f32[128,128]{1,0:T(8,128)S(1)}, f32[128,128]{1,0:T(8,128)}, u32[]{:S(2)}) copy-start(f32[128,128]{1,0:T(8,128)} %cur_ref.1) | copy-start | bytes 196612
  109.4 0.6 copy-start.4
  171.3 31.1 %copy-start.5 = (f32[128,128]{1,0:T(8,128)S(1)}, f32[128,128]{1,0:T(8,128)}, u32[]{:S(2)}) copy-start(f32[128,128]{1,0:T(8,128)} %copy-done.4) | copy-start | bytes 196612

commit v2 on v0

v2 whole, which is shorter than its diff:
```python
import functools
import math

import jax
import jax.numpy as jnp
from jax import lax
from jax.experimental import pallas as pl
from jax.experimental.pallas import tpu as pltpu
from jax.sharding import PartitionSpec as P

ITERS = 2
NX = 4
CORES = 2
UNROLL = 8
SIDES, ACROSS = (1, 3), 2

SMEM = pl.BlockSpec(memory_space=pltpu.SMEM)
VMEM = pl.BlockSpec(memory_space=pltpu.VMEM)
BF16, F32 = jnp.bfloat16, jnp.float32

ROOM = 128
TILE, SLOT, ROW, START, STEPS, SEND, TAKE, TABLE = 0, ROOM, 2 * ROOM, 384, 392, 400, 416, 512


def group_of(block, me):
    return lax.rem(lax.rem(block, NX) - me + NX, NX)


def table_kernel(own, ny, nz, slot_ref, block_ref, ray_ref, tab):
    tiles, slots = slot_ref.shape[0], ray_ref.shape[0]
    here, me = lax.axis_index("space"), lax.rem(lax.axis_index("angle"), NX)
    y, core = here // CORES, lax.rem(here, CORES)
    zero = jnp.int32(0)

    def clear(i, carry):
        for u in range(UNROLL):
            tab[TILE + i * UNROLL + u] = zero
            tab[SLOT + i * UNROLL + u] = jnp.int32(slots)
            tab[ROW + i * UNROLL + u] = jnp.int32(nz)
        return carry

    lax.fori_loop(0, ROOM // UNROLL, clear, 0)

    def count(i, counts):
        for u in range(4):
            d = group_of(block_ref[i * 4 + u], me)
            counts = tuple(c + (d == g).astype(jnp.int32) for g, c in enumerate(counts))
        return counts

    counts = lax.fori_loop(0, tiles // 4, count, (zero,) * NX)
    starts, at = [], zero
    for g in range(NX):
        steps = (counts[g] + UNROLL - 1) // UNROLL
        starts.append(at)
        tab[START + g] = at
        tab[STEPS + g] = steps
        at = at + steps * UNROLL

    def place(i, cursors):
        for u in range(4):
            t = i * 4 + u
            b = block_ref[t]
            d = group_of(b, me)
            seat = cursors[0]
            for g in range(1, NX):
                seat = jnp.where(d == g, cursors[g], seat)
            tab[TILE + seat] = t
            tab[SLOT + seat] = slot_ref[t]
            tab[ROW + seat] = b // NX
            cursors = tuple(c + (d == g).astype(jnp.int32) for g, c in enumerate(cursors))
        return cursors

    lax.fori_loop(0, tiles // 4, place, tuple(starts))
    for j in range(slots):
        ray = ray_ref[j]
        owner = ray // own
        o = ray - owner * own
        theirs = owner // CORES
        side = jnp.where(lax.rem(owner, CORES) == core, 0, ny)
        tab[SEND + j] = (side + lax.rem(theirs - y + ny, ny)) * own + o
        tab[TAKE + j] = (side + lax.rem(y - theirs + ny, ny)) * own + o


def sweep(tab, group, body):
    start = tab[START + group]

    def step(i, carry):
        for u in range(UNROLL):
            at = start + i * UNROLL + u
            body(tab[TILE + at], tab[SLOT + at], tab[ROW + at])
        return carry

    lax.fori_loop(0, tab[STEPS + group], step, 0)


def forward_kernel(groups, first, last, tab, tiles_ref, *refs):
    columns, refs = refs[: len(groups)], refs[len(groups) :]
    before, outs, acc = refs[: 1 - first], refs[1 - first : -1], refs[-1]
    slots = acc.shape[0] - 1
    if first:
        acc[...] = jnp.zeros_like(acc)
    else:
        acc[:slots] = before[0][...]
        acc[slots] = jnp.zeros_like(acc[slots])
    for group, column in zip(groups, columns):

        def body(t, j, z):
            pixels = column[jnp.minimum(z, column.shape[0] - 1)]
            acc[j] += jnp.dot(tiles_ref[t], pixels, preferred_element_type=F32)

        sweep(tab, group, body)
    if not last:
        outs[0][...] = acc[:slots]
        return
    half = outs[0].shape[0]
    for out in outs:
        out[...] = jnp.zeros_like(out)
    for j in range(slots):
        seat = tab[SEND + j]

        @pl.when(seat < half)
        def _():
            outs[0][seat] = acc[j].astype(BF16)

        @pl.when(seat >= half)
        def _():
            outs[1][seat - half] = acc[j].astype(BF16)


def merge_kernel(own, mine_ref, other_ref, near_ref, *far_refs):
    near_ref[...] = mine_ref[:own].astype(F32) + other_ref[:own].astype(F32)
    for d, ref in enumerate(far_refs, 1):
        rows = slice(d * own, (d + 1) * own)
        ref[...] = (mine_ref[rows].astype(F32) + other_ref[rows].astype(F32)).astype(BF16)


def owner_kernel(obs_ref, scale_ref, near_ref, *refs):
    far, (res_ref, flip_ref) = refs[:-2], refs[-2:]
    for o in range(obs_ref.shape[0]):
        total = near_ref[o]
        for ref in far:
            total += ref[o].astype(F32)
        value = scale_ref[o].astype(F32) * (total - obs_ref[o].astype(F32))
        res_ref[o] = value.astype(BF16)
        flip_ref[o] = value.T.astype(BF16)


def backward_kernel(groups, first, tab, tiles_ref, *refs):
    acc = refs[-1]
    if first:
        rays = refs[-2]
        ins, outs, mine_ref = refs[: -3 - len(groups)], refs[-3 - len(groups) : -3], refs[-3]
        own = ins[0].shape[0]
        for n, ref in enumerate(ins):
            rays[n * own : (n + 1) * own] = ref[...]
        for j in range(mine_ref.shape[0]):
            mine_ref[j] = rays[tab[TAKE + j]]
    else:
        mine_ref, outs = refs[0], refs[1:-1]
    slots, nz = mine_ref.shape[0], outs[0].shape[0]
    for group, out in zip(groups, outs):
        acc[...] = jnp.zeros_like(acc)

        def body(t, j, z):
            rays = mine_ref[jnp.minimum(j, slots - 1)]
            acc[z] += jnp.dot(rays, tiles_ref[t], preferred_element_type=F32)

        sweep(tab, group, body)
        out[...] = acc[:nz].astype(BF16)


def sum_kernel(*refs):
    total = refs[0][...].astype(F32)
    for ref in refs[1:-1]:
        total += ref[...].astype(F32)
    refs[-1][...] = total.astype(BF16)


def update_kernel(step_size, grad_ref, cur_ref, new_ref, *copies):
    total = grad_ref[0].astype(F32)
    for k in range(1, grad_ref.shape[0]):
        total += grad_ref[k].astype(F32)
    new = jnp.maximum(cur_ref[...] - step_size * total.T, 0.0)
    new_ref[...] = new
    for copy in copies:
        value = new.astype(BF16)
        for k in range(copy.shape[0]):
            copy[k] = value


def call(kernel, shapes, specs, mib, scratch=(), out=VMEM, work=0):
    return pl.pallas_call(
        kernel,
        out_shape=tuple(jax.ShapeDtypeStruct(shape, dtype) for shape, dtype in shapes),
        in_specs=specs,
        out_specs=(out,) * len(shapes),
        scratch_shapes=list(scratch),
        compiler_params=pltpu.CompilerParams(vmem_limit_bytes=mib << 20),
        cost_estimate=pl.CostEstimate(flops=work, transcendentals=0, bytes_accessed=2 << 20),
    )


def shards(image, tiles, tile_slot, tile_block, slot_ray, sinogram, weights):
    n_space = lax.axis_size("space")
    n_angle = lax.axis_size("angle")
    nz, ny = n_angle // NX, n_space // CORES
    z_groups = [[z * NX + x for z in range(nz)] for x in range(NX)]
    tile_mats = tiles[0]
    own = sinogram.shape[1]
    edge = tile_mats.shape[1]
    slices = image.shape[1]
    blocks = image.shape[0] * n_angle // edge
    slots = slot_ray.shape[1]
    count = tile_slot.shape[1]
    step_size = 0.2 * math.sqrt(blocks / (n_angle * own))
    tile = (edge, slices)
    quarter = 2 * edge * edge * slices * count // NX
    sums = pltpu.VMEM((slots + 1, *tile), F32)
    block_sums = pltpu.VMEM((nz + 1, *tile), F32)

    def along_x(value, d):
        return lax.ppermute(value, "angle", [(i, i // NX * NX + (i + d) % NX) for i in range(n_angle)])

    def along_y(value, d):
        return lax.ppermute(value, "space", [(i, (i + d * CORES) % n_space) for i in range(n_space)])

    def across(value):
        return lax.ppermute(value, "space", [(i, i ^ 1) for i in range(n_space)])

    def along_z(value):
        return lax.all_to_all(value, "angle", 0, 0, axis_index_groups=z_groups, tiled=True)

    def iterate(iteration, current, copies, table):
        column = along_z(copies)
        if table is None:
            (table,) = call(
                functools.partial(table_kernel, own, ny, nz),
                [((TABLE,), jnp.int32)],
                [SMEM] * 3,
                4,
                out=SMEM,
                work=quarter,
            )(tile_slot[0], tile_block[0], slot_ray[0])
        lists = (table, tile_mats)
        columns = {d: along_x(column, d) for d in (*SIDES, ACROSS)}

        def project(distances, before=None):
            first, last = before is None, ACROSS in distances
            received = [column if d == 0 else columns[d] for d in distances]
            return call(
                functools.partial(forward_kernel, [(NX - d) % NX for d in distances], first, last),
                [((ny * own, *tile), BF16)] * 2 if last else [((slots, *tile), F32)],
                [SMEM] + [VMEM] * (1 + len(distances) + (not first)),
                12,
                [sums],
                work=quarter * len(distances),
            )(*lists, *received, *(() if first else (before,)))

        (partial,) = project((0,))
        (partial,) = project(SIDES, partial)
        mine, other = project((ACROSS,), partial)
        near, *far = call(
            functools.partial(merge_kernel, own),
            [((own, *tile), F32)] + [((own, *tile), BF16)] * (ny - 1),
            [VMEM] * 2,
            8,
        )(mine, across(other))
        residual, flipped = call(
            owner_kernel, [((own, *tile), BF16)] * 2, [VMEM] * (2 + ny), 8
        )(sinogram[0], weights[0], near, *[along_y(far[d - 1], d) for d in range(1, ny)])
        same = [flipped] + [along_y(flipped, d) for d in range(1, ny)]
        rays = same + [across(value) for value in same]

        def backproject(groups, operands, first):
            return call(
                functools.partial(backward_kernel, groups, first),
                [((nz, *tile), BF16)] * len(groups) + [((slots, *tile), BF16)] * first,
                [SMEM] + [VMEM] * (1 + len(operands)),
                12,
                [pltpu.VMEM((n_space * own, *tile), BF16)] * first + [block_sums],
                work=quarter * len(groups),
            )(*lists, *operands)

        *parts, slot_res = backproject(SIDES, rays, True)
        summed = [along_x(part, d) for d, part in zip(SIDES, parts)]
        (part,) = backproject((ACROSS,), [slot_res], False)
        summed.append(along_x(part, ACROSS))
        (part,) = backproject((0,), [slot_res], False)
        (column,) = call(sum_kernel, [((nz, *tile), BF16)], [VMEM] * NX, 8)(part, *summed)
        terms = along_z(column)
        more = iteration + 1 < ITERS
        current, *rest = call(
            functools.partial(update_kernel, step_size),
            [(tile, F32)] + [((nz, *tile), BF16)] * more,
            [VMEM] * 2,
            8,
        )(terms, current)
        return (current, residual, rest[0] if more else None, table)

    current, table = image, None
    copies = jnp.broadcast_to(image.astype(BF16)[None], (nz, *tile))
    for iteration in range(ITERS):
        current, residual, copies, table = iterate(iteration, current, copies, table)
    return (current, residual[None])


def solution(mesh):
    placed = (
        P(("space", "angle"), None),
        P("space", "angle", None, None),
        P("space", "angle"),
        P("space", "angle"),
        P("space", "angle"),
        P("angle", "space", None, None),
        P("angle", "space", None, None),
    )
    return jax.shard_map(
        shards,
        mesh=mesh,
        in_specs=placed,
        out_specs=(P(("space", "angle"), None), P("angle", "space", None, None)),
        check_vma=False,
    )
```

time: 828 us -> 195 us (0.24)
  the two profiles are of different devices: /device:TPU:8 before, /device:TPU:1 now
where the time goes in v2:
time: 195 us
  blocking collectives  58.8 us (30%)
  starting transfers between devices  55.3 us (28%)
  waiting for transfers between devices  47.8 us (25%)
  Pallas kernels  27.4 us (14%)
  local copies, waits for them, and re-layouts  3.9 us (2%)
    all_to_all x4, blocking collectives, along_z(): lax.all_to_all(value, 'angle', 0, 0, axis_index_groups=z_groups, tiled=True)  58.8 us
    ppermute x12, waiting for transfers between devices, along_x(): lax.ppermute(value, 'angle', [(i, i // NX * NX + (i + d) % NX) for i in r...  26.2 us
    ppermute x10, starting transfers between devices, across(): return lax.ppermute(value, 'space', [(i, i ^ 1) for i in range(n_space)])  21.1 us
    ppermute x12, starting transfers between devices, along_x(): lax.ppermute(value, 'angle', [(i, i // NX * NX + (i + d) % NX) for i in r...  20.3 us
    ppermute x12, waiting for transfers between devices, along_y(): lax.ppermute(value, 'space', [(i, (i + d * CORES) % n_space) for i in ran...  16.6 us
    ppermute x12, starting transfers between devices, along_y(): lax.ppermute(value, 'space', [(i, (i + d * CORES) % n_space) for i in ran...  13.9 us
    pallas_call x6, Pallas kernels, project(): call(functools.partial(forward_kernel, [(NX - d) % NX for d in distances]...  10.3 us
    pallas_call x6, Pallas kernels, backproject(): call(functools.partial(backward_kernel, groups, first), [((nz, *tile), BF...  10.1 us
  transfers between devices with their start and end apart: 34, of which 18 were waited for; matrix products, arithmetic and copies ran while one was open for 0% of the time, Pallas kernels for 7%

profile of v2, /device:TPU:1, one launch (start us, length us, event | category | flops | bytes accessed | tf_op | source)
XLA Modules:
  0.0 194.9 jit_solution(5884819922342700290)
XLA Ops:
  1.5 19.3 %all_to_all.20.refs_0_ = bf16[8,128,128]{2,1,0:T(8,128)(2,1)S(1)} all-to-all(bf16[8,128,128]{2,1,0:T(8,128)(2,1)S(1)} %broadcast_in_dim.4), channel_id=1, replica_groups={{0,4,8,12,16,20,24,28},{1,5,9,13,17,21,25,29},{2,6,10,14,18,22,26,30},{..., dimensions={0} | all-to-all | bytes 524288 | tf_op jit(solution)/shard_map/all_to_all | solution.py:231
  20.8 2.5 %collective-permute-start.2 = (bf16[8,128,128]{2,1,0:T(8,128)(2,1)S(1)}, bf16[8,128,128]{2,1,0:T(8,128)(2,1)S(1)}, u32[]{:S(2)}, u32[]{:S(2)}) collective-permute-start(bf16[8,128,128]{2,1,0:T(8,128)(2,1)S(1)} %all_to_all.20.refs_0_), channel_id=1, source_target_pairs={{0,3},{1,0},{2,1},{3,2},{4,7},{5,4},{6,5},{7,6},{8,11},{9,8},{10,9... | collective-permute-start | bytes 786440 | tf_op jit(solution)/shard_map/ppermute | solution.py:222
  27.0 4.1 %shard_map.86.tab = s32[512]{0:T(512)S(1)} custom-call(s32[96]{0:T(128)S(1)} %bitcast.23, s32[96]{0:T(128)S(1)} %bitcast.24, s32[8]{0:T(128)S(1)} %bitcast.25), custom_call_target="tpu_custom_call" | custom-call | flops 100663296 | bytes 2097152 | tf_op jit(solution)/shard_map/pallas_call | solution.py:236
  34.4 2.3 %shard_map.88.refs_1_ = f32[8,128,128]{2,1,0:T(8,128)S(1)} custom-call(s32[512]{0:T(512)S(1)} %shard_map.86.tab, bf16[96,128,128]{2,1,0:T(8,128)(2,1)S(1)} %bitcast.8, bf16[8,128,128]{2,1,0:T(8,128)(2,1)S(1)} %collective-permute-done.1.refs_0_, bf16[8,128,128]{2,1,0:T(8,128)(2,1)S(1)} %collective-permute-done.2.refs_1_, f32[8,128,128]{2,1,0:T(8,128)S(1)} %shard_map.87.refs_2_), custom_call_target="tpu_custom_call" | custom-call | flops 201326592 | bytes 2097152 | tf_op jit(solution)/shard_map/pallas_call | solution.py:250
  38.3 4.6 %collective-permute-start.3 = (bf16[16,128,128]{2,1,0:T(8,128)(2,1)S(1)}, bf16[16,128,128]{2,1,0:T(8,128)(2,1)S(1)}, u32[]{:S(2)}, u32[]{:S(2)}) collective-permute-start(bf16[16,128,128]{2,1,0:T(8,128)(2,1)S(1)} %get-tuple-element.26), channel_id=1, source_target_pairs={{0,32},{32,0},{64,96},{96,64},{128,160},{160,128},{192,224},{224,1... | collective-permute-start | bytes 1572872 | tf_op jit(solution)/shard_map/ppermute | solution.py:228
  45.9 2.6 %collective-permute-start.5 = (bf16[4,128,128]{2,1,0:T(8,128)(2,1)S(1)}, bf16[4,128,128]{2,1,0:T(8,128)(2,1)S(1)}, u32[]{:S(2)}, u32[]{:S(2)}) collective-permute-start(bf16[4,128,128]{2,1,0:T(8,128)(2,1)S(1)} %get-tuple-element.29), channel_id=1, source_target_pairs={{0,128},{32,160},{64,192},{96,224},{128,0},{160,32},{192,64},{224,... | collective-permute-start | bytes 393224 | tf_op jit(solution)/shard_map/ppermute | solution.py:225
  50.6 3.9 %collective-permute-done.5.refs_1_ = bf16[4,128,128]{2,1,0:T(8,128)(2,1)S(1)} collective-permute-done((bf16[4,128,128]{2,1,0:T(8,128)(2,1)S(1)}, bf16[4,128,128]{2,1,0:T(8,128)(2,1)S(1)}, u32[]{:S(2)}, u32[]{:S(2)}) %collective-permute-start.5) | collective-permute-done | bytes 131104 | tf_op jit(solution)/shard_map/ppermute | solution.py:225
  55.3 2.2 %collective-permute-start.9 = (bf16[4,128,128]{2,1,0:T(8,128)(2,1)S(1)}, bf16[4,128,128]{2,1,0:T(8,128)(2,1)S(1)}, u32[]{:S(2)}, u32[]{:S(2)}) collective-permute-start(bf16[4,128,128]{2,1,0:T(8,128)(2,1)S(1)} %get-tuple-element.31.refs_0_), channel_id=1, source_target_pairs={{0,192},{32,224},{64,0},{96,32},{128,64},{160,96},{192,128},{224,1... | collective-permute-start | bytes 393224 | tf_op jit(solution)/shard_map/ppermute | solution.py:225
  58.3 1.9 collective-permute-start.10
  61.3 2.7 %collective-permute-start.13 = (bf16[4,128,128]{2,1,0:T(8,128)(2,1)S(1)}, bf16[4,128,128]{2,1,0:T(8,128)(2,1)S(1)}, u32[]{:S(2)}, u32[]{:S(2)}) collective-permute-start(bf16[4,128,128]{2,1,0:T(8,128)(2,1)S(1)} %collective-permute-done.9.refs_3_), channel_id=1, source_target_pairs={{0,32},{32,0},{64,96},{96,64},{128,160},{160,128},{192,224},{224,1... | collective-permute-start | bytes 393224 | tf_op jit(solution)/shard_map/ppermute | solution.py:228
  64.0 2.3 %collective-permute-start.12 = (bf16[4,128,128]{2,1,0:T(8,128)(2,1)S(1)}, bf16[4,128,128]{2,1,0:T(8,128)(2,1)S(1)}, u32[]{:S(2)}, u32[]{:S(2)}) collective-permute-start(bf16[4,128,128]{2,1,0:T(8,128)(2,1)S(1)} %collective-permute-done.8.refs_2_), channel_id=1, source_target_pairs={{0,32},{32,0},{64,96},{96,64},{128,160},{160,128},{192,224},{224,1... | collective-permute-start | bytes 393224 | tf_op jit(solution)/shard_map/ppermute | solution.py:228
  68.7 2.4 %shard_map.92 = (bf16[8,128,128]{2,1,0:T(8,128)(2,1)S(1)}, bf16[8,128,128]{2,1,0:T(8,128)(2,1)S(1)}, bf16[8,128,128]{2,1,0:T(8,128)(2,1)S(1)}) custom-call(s32[512]{0:T(512)S(1)} %shard_map.86.tab, bf16[96,128,128]{2,1,0:T(8,128)(2,1)S(1)} %bitcast.10, bf16[4,128,128]{2,1,0:T(8,128)(2,1)S(1)} %get-tuple-element.31.refs_0_, ...), custom_call_target="tpu_custom_call" | custom-call | flops 201326592 | bytes 2097152 | tf_op jit(solution)/shard_map/pallas_call | solution.py:275
  73.5 2.3 %collective-permute-start.15 = (bf16[8,128,128]{2,1,0:T(8,128)(2,1)S(1)}, bf16[8,128,128]{2,1,0:T(8,128)(2,1)S(1)}, u32[]{:S(2)}, u32[]{:S(2)}) collective-permute-start(bf16[8,128,128]{2,1,0:T(8,128)(2,1)S(1)} %get-tuple-element.34), channel_id=1, source_target_pairs={{0,3},{1,0},{2,1},{3,2},{4,7},{5,4},{6,5},{7,6},{8,11},{9,8},{10,9... | collective-permute-start | bytes 786440 | tf_op jit(solution)/shard_map/ppermute | solution.py:222
  77.1 4.7 %collective-permute-done.16.refs_3_ = bf16[8,128,128]{2,1,0:T(8,128)(2,1)S(1)} collective-permute-done((bf16[8,128,128]{2,1,0:T(8,128)(2,1)S(1)}, bf16[8,128,128]{2,1,0:T(8,128)(2,1)S(1)}, u32[]{:S(2)}, u32[]{:S(2)}) %collective-permute-start.16) | collective-permute-done | bytes 262176 | tf_op jit(solution)/shard_map/ppermute | solution.py:222
  81.8 6.3 %collective-permute-done.14.refs_1_ = bf16[8,128,128]{2,1,0:T(8,128)(2,1)S(1)} collective-permute-done((bf16[8,128,128]{2,1,0:T(8,128)(2,1)S(1)}, bf16[8,128,128]{2,1,0:T(8,128)(2,1)S(1)}, u32[]{:S(2)}, u32[]{:S(2)}) %collective-permute-start.14) | collective-permute-done | bytes 262176 | tf_op jit(solution)/shard_map/ppermute | solution.py:222
  88.2 13.2 %all_to_all.21.grad_ref = bf16[8,128,128]{2,1,0:T(8,128)(2,1)S(1)} all-to-all(bf16[8,128,128]{2,1,0:T(8,128)(2,1)S(1)} %shard_map.95), channel_id=1, replica_groups={{0,4,8,12,16,20,24,28},{1,5,9,13,17,21,25,29},{2,6,10,14,18,22,26,30},{..., dimensions={0} | all-to-all | bytes 524288 | tf_op jit(solution)/shard_map/all_to_all | solution.py:231
  101.6 11.6 %all_to_all.22.refs_0_ = bf16[8,128,128]{2,1,0:T(8,128)(2,1)S(1)} all-to-all(bf16[8,128,128]{2,1,0:T(8,128)(2,1)S(1)} %get-tuple-element.35), channel_id=1, replica_groups={{0,4,8,12,16,20,24,28},{1,5,9,13,17,21,25,29},{2,6,10,14,18,22,26,30},{..., dimensions={0} | all-to-all | bytes 524288 | tf_op jit(solution)/shard_map/all_to_all | solution.py:231
  113.3 3.9 %collective-permute-start.18 = (bf16[8,128,128]{2,1,0:T(8,128)(2,1)S(1)}, bf16[8,128,128]{2,1,0:T(8,128)(2,1)S(1)}, u32[]{:S(2)}, u32[]{:S(2)}) collective-permute-start(bf16[8,128,128]{2,1,0:T(8,128)(2,1)S(1)} %all_to_all.22.refs_0_), channel_id=1, source_target_pairs={{0,1},{1,2},{2,3},{3,0},{4,5},{5,6},{6,7},{7,4},{8,9},{9,10},{10,1... | collective-permute-start | bytes 786440 | tf_op jit(solution)/shard_map/ppermute | solution.py:222
  120.3 1.9 collective-permute-done.19.refs_1_
  122.2 2.3 %shard_map.98.refs_1_ = f32[8,128,128]{2,1,0:T(8,128)S(1)} custom-call(s32[512]{0:T(512)S(1)} %shard_map.86.tab, bf16[96,128,128]{2,1,0:T(8,128)(2,1)S(1)} %bitcast.14, bf16[8,128,128]{2,1,0:T(8,128)(2,1)S(1)} %collective-permute-done.18.refs_0_, bf16[8,128,128]{2,1,0:T(8,128)(2,1)S(1)} %collective-permute-done.19.refs_1_, f32[8,128,128]{2,1,0:T(8,128)S(1)} %shard_map.97.refs_2_), custom_call_target="tpu_custom_call" | custom-call | flops 201326592 | bytes 2097152 | tf_op jit(solution)/shard_map/pallas_call | solution.py:250
  124.5 4.9 %collective-permute-done.17.refs_0_ = bf16[8,128,128]{2,1,0:T(8,128)(2,1)S(1)} collective-permute-done((bf16[8,128,128]{2,1,0:T(8,128)(2,1)S(1)}, bf16[8,128,128]{2,1,0:T(8,128)(2,1)S(1)}, u32[]{:S(2)}, u32[]{:S(2)}) %collective-permute-start.17) | collective-permute-done | bytes 262176 | tf_op jit(solution)/shard_map/ppermute | solution.py:222
  131.0 2.8 %collective-permute-start.20 = (bf16[16,128,128]{2,1,0:T(8,128)(2,1)S(1)}, bf16[16,128,128]{2,1,0:T(8,128)(2,1)S(1)}, u32[]{:S(2)}, u32[]{:S(2)}) collective-permute-start(bf16[16,128,128]{2,1,0:T(8,128)(2,1)S(1)} %get-tuple-element.37), channel_id=1, source_target_pairs={{0,32},{32,0},{64,96},{96,64},{128,160},{160,128},{192,224},{224,1... | collective-permute-start | bytes 1572872 | tf_op jit(solution)/shard_map/ppermute | solution.py:228
  138.2 6.2 %collective-permute-done.21.refs_0_ = bf16[4,128,128]{2,1,0:T(8,128)(2,1)S(1)} collective-permute-done((bf16[4,128,128]{2,1,0:T(8,128)(2,1)S(1)}, bf16[4,128,128]{2,1,0:T(8,128)(2,1)S(1)}, u32[]{:S(2)}, u32[]{:S(2)}) %collective-permute-start.21) | collective-permute-done | bytes 131104 | tf_op jit(solution)/shard_map/ppermute | solution.py:225
  145.4 2.7 %collective-permute-start.26 = (bf16[4,128,128]{2,1,0:T(8,128)(2,1)S(1)}, bf16[4,128,128]{2,1,0:T(8,128)(2,1)S(1)}, u32[]{:S(2)}, u32[]{:S(2)}) collective-permute-start(bf16[4,128,128]{2,1,0:T(8,128)(2,1)S(1)} %get-tuple-element.42.refs_0_), channel_id=1, source_target_pairs={{0,192},{32,224},{64,0},{96,32},{128,64},{160,96},{192,128},{224,1... | collective-permute-start | bytes 393224 | tf_op jit(solution)/shard_map/ppermute | solution.py:225
  150.0 3.3 %collective-permute-done.26.refs_3_ = bf16[4,128,128]{2,1,0:T(8,128)(2,1)S(1)} collective-permute-done((bf16[4,128,128]{2,1,0:T(8,128)(2,1)S(1)}, bf16[4,128,128]{2,1,0:T(8,128)(2,1)S(1)}, u32[]{:S(2)}, u32[]{:S(2)}) %collective-permute-start.26) | collective-permute-done | bytes 131104 | tf_op jit(solution)/shard_map/ppermute | solution.py:225
  154.7 2.3 %collective-permute-start.29 = (bf16[4,128,128]{2,1,0:T(8,128)(2,1)S(1)}, bf16[4,128,128]{2,1,0:T(8,128)(2,1)S(1)}, u32[]{:S(2)}, u32[]{:S(2)}) collective-permute-start(bf16[4,128,128]{2,1,0:T(8,128)(2,1)S(1)} %collective-permute-done.25.refs_2_), channel_id=1, source_target_pairs={{0,32},{32,0},{64,96},{96,64},{128,160},{160,128},{192,224},{224,1... | collective-permute-start | bytes 393224 | tf_op jit(solution)/shard_map/ppermute | solution.py:228
  159.0 2.4 %shard_map.102 = (bf16[8,128,128]{2,1,0:T(8,128)(2,1)S(1)}, bf16[8,128,128]{2,1,0:T(8,128)(2,1)S(1)}, bf16[8,128,128]{2,1,0:T(8,128)(2,1)S(1)}) custom-call(s32[512]{0:T(512)S(1)} %shard_map.86.tab, bf16[96,128,128]{2,1,0:T(8,128)(2,1)S(1)} %bitcast.16, bf16[4,128,128]{2,1,0:T(8,128)(2,1)S(1)} %get-tuple-element.42.refs_0_, ...), custom_call_target="tpu_custom_call" | custom-call | flops 201326592 | bytes 2097152 | tf_op jit(solution)/shard_map/pallas_call | solution.py:275
  162.8 4.3 %collective-permute-start.33 = (bf16[8,128,128]{2,1,0:T(8,128)(2,1)S(1)}, bf16[8,128,128]{2,1,0:T(8,128)(2,1)S(1)}, u32[]{:S(2)}, u32[]{:S(2)}) collective-permute-start(bf16[8,128,128]{2,1,0:T(8,128)(2,1)S(1)} %shard_map.104), channel_id=1, source_target_pairs={{0,2},{1,3},{2,0},{3,1},{4,6},{5,7},{6,4},{7,5},{8,10},{9,11},{10,... | collective-permute-start | bytes 786440 | tf_op jit(solution)/shard_map/ppermute | solution.py:222
  167.0 2.7 %collective-permute-start.32 = (bf16[8,128,128]{2,1,0:T(8,128)(2,1)S(1)}, bf16[8,128,128]{2,1,0:T(8,128)(2,1)S(1)}, u32[]{:S(2)}, u32[]{:S(2)}) collective-permute-start(bf16[8,128,128]{2,1,0:T(8,128)(2,1)S(1)} %get-tuple-element.45), channel_id=1, source_target_pairs={{0,3},{1,0},{2,1},{3,2},{4,7},{5,4},{6,5},{7,6},{8,11},{9,8},{10,9... | collective-permute-start | bytes 786440 | tf_op jit(solution)/shard_map/ppermute | solution.py:222
  171.0 2.6 %collective-permute-done.33.refs_3_ = bf16[8,128,128]{2,1,0:T(8,128)(2,1)S(1)} collective-permute-done((bf16[8,128,128]{2,1,0:T(8,128)(2,1)S(1)}, bf16[8,128,128]{2,1,0:T(8,128)(2,1)S(1)}, u32[]{:S(2)}, u32[]{:S(2)}) %collective-permute-start.33) | collective-permute-done | bytes 262176 | tf_op jit(solution)/shard_map/ppermute | solution.py:222
  173.6 5.8 %collective-permute-done.31.refs_1_ = bf16[8,128,128]{2,1,0:T(8,128)(2,1)S(1)} collective-permute-done((bf16[8,128,128]{2,1,0:T(8,128)(2,1)S(1)}, bf16[8,128,128]{2,1,0:T(8,128)(2,1)S(1)}, u32[]{:S(2)}, u32[]{:S(2)}) %collective-permute-start.31) | collective-permute-done | bytes 262176 | tf_op jit(solution)/shard_map/ppermute | solution.py:222
  179.6 14.6 %all_to_all.23.grad_ref = bf16[8,128,128]{2,1,0:T(8,128)(2,1)S(1)} all-to-all(bf16[8,128,128]{2,1,0:T(8,128)(2,1)S(1)} %shard_map.105), channel_id=1, replica_groups={{0,4,8,12,16,20,24,28},{1,5,9,13,17,21,25,29},{2,6,10,14,18,22,26,30},{..., dimensions={0} | all-to-all | bytes 524288 | tf_op jit(solution)/shard_map/all_to_all | solution.py:231
  (77 shorter events, 42.5 us)
Async XLA Ops:
  20.8 13.5 %collective-permute-start.2 = (bf16[8,128,128]{2,1,0:T(8,128)(2,1)S(1)}, bf16[8,128,128]{2,1,0:T(8,128)(2,1)S(1)}, u32[]{:S(2)}, u32[]{:S(2)}) collective-permute-start(bf16[8,128,128]{2,1,0:T(8,128)(2,1)S(1)} %all_to_all.20.refs_0_), channel_id=1, source_target_pairs={{0,3},{1,0},{2,1},{3,2},{4,7},{5,4},{6,5},{7,6},{8,11},{9,8},{10,9... | collective-permute-start | bytes 786440 | tf_op jit(solution)/shard_map/ppermute | solution.py:222
  23.3 11.1 %collective-permute-start.1 = (bf16[8,128,128]{2,1,0:T(8,128)(2,1)S(1)}, bf16[8,128,128]{2,1,0:T(8,128)(2,1)S(1)}, u32[]{:S(2)}, u32[]{:S(2)}) collective-permute-start(bf16[8,128,128]{2,1,0:T(8,128)(2,1)S(1)} %all_to_all.20.refs_0_), channel_id=1, source_target_pairs={{0,1},{1,2},{2,3},{3,0},{4,5},{5,6},{6,7},{7,4},{8,9},{9,10},{10,1... | collective-permute-start | bytes 786440 | tf_op jit(solution)/shard_map/ppermute | solution.py:222
  23.3 13.4 %collective-permute-start = (bf16[8,128,128]{2,1,0:T(8,128)(2,1)S(1)}, bf16[8,128,128]{2,1,0:T(8,128)(2,1)S(1)}, u32[]{:S(2)}, u32[]{:S(2)}) collective-permute-start(bf16[8,128,128]{2,1,0:T(8,128)(2,1)S(1)} %all_to_all.20.refs_0_), channel_id=1, source_target_pairs={{0,2},{1,3},{2,0},{3,1},{4,6},{5,7},{6,4},{7,5},{8,10},{9,11},{10,... | collective-permute-start | bytes 786440 | tf_op jit(solution)/shard_map/ppermute | solution.py:222
  38.3 6.1 %collective-permute-start.3 = (bf16[16,128,128]{2,1,0:T(8,128)(2,1)S(1)}, bf16[16,128,128]{2,1,0:T(8,128)(2,1)S(1)}, u32[]{:S(2)}, u32[]{:S(2)}) collective-permute-start(bf16[16,128,128]{2,1,0:T(8,128)(2,1)S(1)} %get-tuple-element.26), channel_id=1, source_target_pairs={{0,32},{32,0},{64,96},{96,64},{128,160},{160,128},{192,224},{224,1... | collective-permute-start | bytes 1572872 | tf_op jit(solution)/shard_map/ppermute | solution.py:228
  44.5 6.1 %collective-permute-start.4 = (bf16[4,128,128]{2,1,0:T(8,128)(2,1)S(1)}, bf16[4,128,128]{2,1,0:T(8,128)(2,1)S(1)}, u32[]{:S(2)}, u32[]{:S(2)}) collective-permute-start(bf16[4,128,128]{2,1,0:T(8,128)(2,1)S(1)} %get-tuple-element.28), channel_id=1, source_target_pairs={{0,64},{32,96},{64,128},{96,160},{128,192},{160,224},{192,0},{224,... | collective-permute-start | bytes 393224 | tf_op jit(solution)/shard_map/ppermute | solution.py:225
  45.9 8.6 %collective-permute-start.5 = (bf16[4,128,128]{2,1,0:T(8,128)(2,1)S(1)}, bf16[4,128,128]{2,1,0:T(8,128)(2,1)S(1)}, u32[]{:S(2)}, u32[]{:S(2)}) collective-permute-start(bf16[4,128,128]{2,1,0:T(8,128)(2,1)S(1)} %get-tuple-element.29), channel_id=1, source_target_pairs={{0,128},{32,160},{64,192},{96,224},{128,0},{160,32},{192,64},{224,... | collective-permute-start | bytes 393224 | tf_op jit(solution)/shard_map/ppermute | solution.py:225
  48.5 6.0 %collective-permute-start.6 = (bf16[4,128,128]{2,1,0:T(8,128)(2,1)S(1)}, bf16[4,128,128]{2,1,0:T(8,128)(2,1)S(1)}, u32[]{:S(2)}, u32[]{:S(2)}) collective-permute-start(bf16[4,128,128]{2,1,0:T(8,128)(2,1)S(1)} %get-tuple-element.30), channel_id=1, source_target_pairs={{0,192},{32,224},{64,0},{96,32},{128,64},{160,96},{192,128},{224,1... | collective-permute-start | bytes 393224 | tf_op jit(solution)/shard_map/ppermute | solution.py:225
  55.3 6.0 %collective-permute-start.9 = (bf16[4,128,128]{2,1,0:T(8,128)(2,1)S(1)}, bf16[4,128,128]{2,1,0:T(8,128)(2,1)S(1)}, u32[]{:S(2)}, u32[]{:S(2)}) collective-permute-start(bf16[4,128,128]{2,1,0:T(8,128)(2,1)S(1)} %get-tuple-element.31.refs_0_), channel_id=1, source_target_pairs={{0,192},{32,224},{64,0},{96,32},{128,64},{160,96},{192,128},{224,1... | collective-permute-start | bytes 393224 | tf_op jit(solution)/shard_map/ppermute | solution.py:225
  57.5 6.6 %collective-permute-start.8 = (bf16[4,128,128]{2,1,0:T(8,128)(2,1)S(1)}, bf16[4,128,128]{2,1,0:T(8,128)(2,1)S(1)}, u32[]{:S(2)}, u32[]{:S(2)}) collective-permute-start(bf16[4,128,128]{2,1,0:T(8,128)(2,1)S(1)} %get-tuple-element.31.refs_0_), channel_id=1, source_target_pairs={{0,128},{32,160},{64,192},{96,224},{128,0},{160,32},{192,64},{224,... | collective-permute-start | bytes 393224 | tf_op jit(solution)/shard_map/ppermute | solution.py:225
  58.3 8.3 %collective-permute-start.7 = (bf16[4,128,128]{2,1,0:T(8,128)(2,1)S(1)}, bf16[4,128,128]{2,1,0:T(8,128)(2,1)S(1)}, u32[]{:S(2)}, u32[]{:S(2)}) collective-permute-start(bf16[4,128,128]{2,1,0:T(8,128)(2,1)S(1)} %get-tuple-element.31.refs_0_), channel_id=1, source_target_pairs={{0,64},{32,96},{64,128},{96,160},{128,192},{160,224},{192,0},{224,... | collective-permute-start | bytes 393224 | tf_op jit(solution)/shard_map/ppermute | solution.py:225
  58.3 9.4 %collective-permute-start.10 = (bf16[4,128,128]{2,1,0:T(8,128)(2,1)S(1)}, bf16[4,128,128]{2,1,0:T(8,128)(2,1)S(1)}, u32[]{:S(2)}, u32[]{:S(2)}) collective-permute-start(bf16[4,128,128]{2,1,0:T(8,128)(2,1)S(1)} %get-tuple-element.31.refs_0_), channel_id=1, source_target_pairs={{0,32},{32,0},{64,96},{96,64},{128,160},{160,128},{192,224},{224,1... | collective-permute-start | bytes 393224 | tf_op jit(solution)/shard_map/ppermute | solution.py:228
  61.3 6.4 %collective-permute-start.13 = (bf16[4,128,128]{2,1,0:T(8,128)(2,1)S(1)}, bf16[4,128,128]{2,1,0:T(8,128)(2,1)S(1)}, u32[]{:S(2)}, u32[]{:S(2)}) collective-permute-start(bf16[4,128,128]{2,1,0:T(8,128)(2,1)S(1)} %collective-permute-done.9.refs_3_), channel_id=1, source_target_pairs={{0,32},{32,0},{64,96},{96,64},{128,160},{160,128},{192,224},{224,1... | collective-permute-start | bytes 393224 | tf_op jit(solution)/shard_map/ppermute | solution.py:228
  64.0 3.7 %collective-permute-start.12 = (bf16[4,128,128]{2,1,0:T(8,128)(2,1)S(1)}, bf16[4,128,128]{2,1,0:T(8,128)(2,1)S(1)}, u32[]{:S(2)}, u32[]{:S(2)}) collective-permute-start(bf16[4,128,128]{2,1,0:T(8,128)(2,1)S(1)} %collective-permute-done.8.refs_2_), channel_id=1, source_target_pairs={{0,32},{32,0},{64,96},{96,64},{128,160},{160,128},{192,224},{224,1... | collective-permute-start | bytes 393224 | tf_op jit(solution)/shard_map/ppermute | solution.py:228
  72.5 9.3 %collective-permute-start.16 = (bf16[8,128,128]{2,1,0:T(8,128)(2,1)S(1)}, bf16[8,128,128]{2,1,0:T(8,128)(2,1)S(1)}, u32[]{:S(2)}, u32[]{:S(2)}) collective-permute-start(bf16[8,128,128]{2,1,0:T(8,128)(2,1)S(1)} %shard_map.94), channel_id=1, source_target_pairs={{0,2},{1,3},{2,0},{3,1},{4,6},{5,7},{6,4},{7,5},{8,10},{9,11},{10,... | collective-permute-start | bytes 786440 | tf_op jit(solution)/shard_map/ppermute | solution.py:222
  73.0 15.0 %collective-permute-start.14 = (bf16[8,128,128]{2,1,0:T(8,128)(2,1)S(1)}, bf16[8,128,128]{2,1,0:T(8,128)(2,1)S(1)}, u32[]{:S(2)}, u32[]{:S(2)}) collective-permute-start(bf16[8,128,128]{2,1,0:T(8,128)(2,1)S(1)} %get-tuple-element.33), channel_id=1, source_target_pairs={{0,1},{1,2},{2,3},{3,0},{4,5},{5,6},{6,7},{7,4},{8,9},{9,10},{10,1... | collective-permute-start | bytes 786440 | tf_op jit(solution)/shard_map/ppermute | solution.py:222
  73.5 14.6 %collective-permute-start.15 = (bf16[8,128,128]{2,1,0:T(8,128)(2,1)S(1)}, bf16[8,128,128]{2,1,0:T(8,128)(2,1)S(1)}, u32[]{:S(2)}, u32[]{:S(2)}) collective-permute-start(bf16[8,128,128]{2,1,0:T(8,128)(2,1)S(1)} %get-tuple-element.34), channel_id=1, source_target_pairs={{0,3},{1,0},{2,1},{3,2},{4,7},{5,4},{6,5},{7,6},{8,11},{9,8},{10,9... | collective-permute-start | bytes 786440 | tf_op jit(solution)/shard_map/ppermute | solution.py:222
  113.2 9.0 %collective-permute-start.19 = (bf16[8,128,128]{2,1,0:T(8,128)(2,1)S(1)}, bf16[8,128,128]{2,1,0:T(8,128)(2,1)S(1)}, u32[]{:S(2)}, u32[]{:S(2)}) collective-permute-start(bf16[8,128,128]{2,1,0:T(8,128)(2,1)S(1)} %all_to_all.22.refs_0_), channel_id=1, source_target_pairs={{0,3},{1,0},{2,1},{3,2},{4,7},{5,4},{6,5},{7,6},{8,11},{9,8},{10,9... | collective-permute-start | bytes 786440 | tf_op jit(solution)/shard_map/ppermute | solution.py:222
  113.3 8.9 %collective-permute-start.18 = (bf16[8,128,128]{2,1,0:T(8,128)(2,1)S(1)}, bf16[8,128,128]{2,1,0:T(8,128)(2,1)S(1)}, u32[]{:S(2)}, u32[]{:S(2)}) collective-permute-start(bf16[8,128,128]{2,1,0:T(8,128)(2,1)S(1)} %all_to_all.22.refs_0_), channel_id=1, source_target_pairs={{0,1},{1,2},{2,3},{3,0},{4,5},{5,6},{6,7},{7,4},{8,9},{9,10},{10,1... | collective-permute-start | bytes 786440 | tf_op jit(solution)/shard_map/ppermute | solution.py:222
  117.2 12.2 %collective-permute-start.17 = (bf16[8,128,128]{2,1,0:T(8,128)(2,1)S(1)}, bf16[8,128,128]{2,1,0:T(8,128)(2,1)S(1)}, u32[]{:S(2)}, u32[]{:S(2)}) collective-permute-start(bf16[8,128,128]{2,1,0:T(8,128)(2,1)S(1)} %all_to_all.22.refs_0_), channel_id=1, source_target_pairs={{0,2},{1,3},{2,0},{3,1},{4,6},{5,7},{6,4},{7,5},{8,10},{9,11},{10,... | collective-permute-start | bytes 786440 | tf_op jit(solution)/shard_map/ppermute | solution.py:222
  131.0 4.4 %collective-permute-start.20 = (bf16[16,128,128]{2,1,0:T(8,128)(2,1)S(1)}, bf16[16,128,128]{2,1,0:T(8,128)(2,1)S(1)}, u32[]{:S(2)}, u32[]{:S(2)}) collective-permute-start(bf16[16,128,128]{2,1,0:T(8,128)(2,1)S(1)} %get-tuple-element.37), channel_id=1, source_target_pairs={{0,32},{32,0},{64,96},{96,64},{128,160},{160,128},{192,224},{224,1... | collective-permute-start | bytes 1572872 | tf_op jit(solution)/shard_map/ppermute | solution.py:228
  135.4 9.0 %collective-permute-start.21 = (bf16[4,128,128]{2,1,0:T(8,128)(2,1)S(1)}, bf16[4,128,128]{2,1,0:T(8,128)(2,1)S(1)}, u32[]{:S(2)}, u32[]{:S(2)}) collective-permute-start(bf16[4,128,128]{2,1,0:T(8,128)(2,1)S(1)} %get-tuple-element.39), channel_id=1, source_target_pairs={{0,64},{32,96},{64,128},{96,160},{128,192},{160,224},{192,0},{224,... | collective-permute-start | bytes 393224 | tf_op jit(solution)/shard_map/ppermute | solution.py:225
  135.5 8.9 %collective-permute-start.22 = (bf16[4,128,128]{2,1,0:T(8,128)(2,1)S(1)}, bf16[4,128,128]{2,1,0:T(8,128)(2,1)S(1)}, u32[]{:S(2)}, u32[]{:S(2)}) collective-permute-start(bf16[4,128,128]{2,1,0:T(8,128)(2,1)S(1)} %get-tuple-element.40), channel_id=1, source_target_pairs={{0,128},{32,160},{64,192},{96,224},{128,0},{160,32},{192,64},{224,... | collective-permute-start | bytes 393224 | tf_op jit(solution)/shard_map/ppermute | solution.py:225
  136.5 8.1 %collective-permute-start.23 = (bf16[4,128,128]{2,1,0:T(8,128)(2,1)S(1)}, bf16[4,128,128]{2,1,0:T(8,128)(2,1)S(1)}, u32[]{:S(2)}, u32[]{:S(2)}) collective-permute-start(bf16[4,128,128]{2,1,0:T(8,128)(2,1)S(1)} %get-tuple-element.41), channel_id=1, source_target_pairs={{0,192},{32,224},{64,0},{96,32},{128,64},{160,96},{192,128},{224,1... | collective-permute-start | bytes 393224 | tf_op jit(solution)/shard_map/ppermute | solution.py:225
  145.4 8.0 %collective-permute-start.26 = (bf16[4,128,128]{2,1,0:T(8,128)(2,1)S(1)}, bf16[4,128,128]{2,1,0:T(8,128)(2,1)S(1)}, u32[]{:S(2)}, u32[]{:S(2)}) collective-permute-start(bf16[4,128,128]{2,1,0:T(8,128)(2,1)S(1)} %get-tuple-element.42.refs_0_), channel_id=1, source_target_pairs={{0,192},{32,224},{64,0},{96,32},{128,64},{160,96},{192,128},{224,1... | collective-permute-start | bytes 393224 | tf_op jit(solution)/shard_map/ppermute | solution.py:225
  148.1 6.6 %collective-permute-start.25 = (bf16[4,128,128]{2,1,0:T(8,128)(2,1)S(1)}, bf16[4,128,128]{2,1,0:T(8,128)(2,1)S(1)}, u32[]{:S(2)}, u32[]{:S(2)}) collective-permute-start(bf16[4,128,128]{2,1,0:T(8,128)(2,1)S(1)} %get-tuple-element.42.refs_0_), channel_id=1, source_target_pairs={{0,128},{32,160},{64,192},{96,224},{128,0},{160,32},{192,64},{224,... | collective-permute-start | bytes 393224 | tf_op jit(solution)/shard_map/ppermute | solution.py:225
  148.1 9.1 %collective-permute-start.24 = (bf16[4,128,128]{2,1,0:T(8,128)(2,1)S(1)}, bf16[4,128,128]{2,1,0:T(8,128)(2,1)S(1)}, u32[]{:S(2)}, u32[]{:S(2)}) collective-permute-start(bf16[4,128,128]{2,1,0:T(8,128)(2,1)S(1)} %get-tuple-element.42.refs_0_), channel_id=1, source_target_pairs={{0,64},{32,96},{64,128},{96,160},{128,192},{160,224},{192,0},{224,... | collective-permute-start | bytes 393224 | tf_op jit(solution)/shard_map/ppermute | solution.py:225
  148.7 9.4 %collective-permute-start.27 = (bf16[4,128,128]{2,1,0:T(8,128)(2,1)S(1)}, bf16[4,128,128]{2,1,0:T(8,128)(2,1)S(1)}, u32[]{:S(2)}, u32[]{:S(2)}) collective-permute-start(bf16[4,128,128]{2,1,0:T(8,128)(2,1)S(1)} %get-tuple-element.42.refs_0_), channel_id=1, source_target_pairs={{0,32},{32,0},{64,96},{96,64},{128,160},{160,128},{192,224},{224,1... | collective-permute-start | bytes 393224 | tf_op jit(solution)/shard_map/ppermute | solution.py:228
  153.3 4.7 %collective-permute-start.30 = (bf16[4,128,128]{2,1,0:T(8,128)(2,1)S(1)}, bf16[4,128,128]{2,1,0:T(8,128)(2,1)S(1)}, u32[]{:S(2)}, u32[]{:S(2)}) collective-permute-start(bf16[4,128,128]{2,1,0:T(8,128)(2,1)S(1)} %collective-permute-done.26.refs_3_), channel_id=1, source_target_pairs={{0,32},{32,0},{64,96},{96,64},{128,160},{160,128},{192,224},{224,1... | collective-permute-start | bytes 393224 | tf_op jit(solution)/shard_map/ppermute | solution.py:228
  154.7 3.4 %collective-permute-start.29 = (bf16[4,128,128]{2,1,0:T(8,128)(2,1)S(1)}, bf16[4,128,128]{2,1,0:T(8,128)(2,1)S(1)}, u32[]{:S(2)}, u32[]{:S(2)}) collective-permute-start(bf16[4,128,128]{2,1,0:T(8,128)(2,1)S(1)} %collective-permute-done.25.refs_2_), channel_id=1, source_target_pairs={{0,32},{32,0},{64,96},{96,64},{128,160},{160,128},{192,224},{224,1... | collective-permute-start | bytes 393224 | tf_op jit(solution)/shard_map/ppermute | solution.py:228
  162.8 10.9 %collective-permute-start.33 = (bf16[8,128,128]{2,1,0:T(8,128)(2,1)S(1)}, bf16[8,128,128]{2,1,0:T(8,128)(2,1)S(1)}, u32[]{:S(2)}, u32[]{:S(2)}) collective-permute-start(bf16[8,128,128]{2,1,0:T(8,128)(2,1)S(1)} %shard_map.104), channel_id=1, source_target_pairs={{0,2},{1,3},{2,0},{3,1},{4,6},{5,7},{6,4},{7,5},{8,10},{9,11},{10,... | collective-permute-start | bytes 786440 | tf_op jit(solution)/shard_map/ppermute | solution.py:222
  167.0 12.4 %collective-permute-start.31 = (bf16[8,128,128]{2,1,0:T(8,128)(2,1)S(1)}, bf16[8,128,128]{2,1,0:T(8,128)(2,1)S(1)}, u32[]{:S(2)}, u32[]{:S(2)}) collective-permute-start(bf16[8,128,128]{2,1,0:T(8,128)(2,1)S(1)} %get-tuple-element.44), channel_id=1, source_target_pairs={{0,1},{1,2},{2,3},{3,0},{4,5},{5,6},{6,7},{7,4},{8,9},{9,10},{10,1... | collective-permute-start | bytes 786440 | tf_op jit(solution)/shard_map/ppermute | solution.py:222
  167.0 12.4 %collective-permute-start.32 = (bf16[8,128,128]{2,1,0:T(8,128)(2,1)S(1)}, bf16[8,128,128]{2,1,0:T(8,128)(2,1)S(1)}, u32[]{:S(2)}, u32[]{:S(2)}) collective-permute-start(bf16[8,128,128]{2,1,0:T(8,128)(2,1)S(1)} %get-tuple-element.45), channel_id=1, source_target_pairs={{0,3},{1,0},{2,1},{3,2},{4,7},{5,4},{6,5},{7,6},{8,11},{9,8},{10,9... | collective-permute-start | bytes 786440 | tf_op jit(solution)/shard_map/ppermute | solution.py:222
  (9 other events, 72.5 us)

commit v3 on v2

v3 whole, which is shorter than its diff:
```python
import functools
import math

import jax
import jax.numpy as jnp
from jax import lax
from jax.experimental import pallas as pl
from jax.experimental.pallas import tpu as pltpu
from jax.sharding import PartitionSpec as P

ITERS = 2
NX = 4
CORES = 2
UNROLL = 26
RIGHT, ACROSS, LEFT = 1, 2, 3

SMEM = pl.BlockSpec(memory_space=pltpu.SMEM)
VMEM = pl.BlockSpec(memory_space=pltpu.VMEM)
HBM = pl.BlockSpec(memory_space=pltpu.HBM)
BF16, F32 = jnp.bfloat16, jnp.float32

ROOM = 128
TILE, SEAT, SLOT, SEND, TAKE, STEPS, TABLE = 0, ROOM, 2 * ROOM, 320, 336, 352, 384


def table_kernel(own, ny, nz, *refs):
    sources, (tab, near_tiles), lists, sems = refs[:4], refs[4:6], refs[6:9], refs[9]
    slot_ref, block_ref, ray_ref = lists
    tiles, slots = slot_ref.shape[0], ray_ref.shape[0]
    targets = (*lists, near_tiles.at[pl.ds(0, tiles)])
    copies = [
        pltpu.make_async_copy(source, target, sems.at[n]) for n, (source, target) in enumerate(zip(sources, targets))
    ]
    for copy in copies:
        copy.start()
    near_tiles[tiles] = jnp.zeros_like(near_tiles[tiles])
    here, me = lax.axis_index("space"), lax.rem(lax.axis_index("angle"), NX)
    y, core = here // CORES, lax.rem(here, CORES)
    zero = jnp.int32(0)

    def clear(i, carry):
        for u in range(8):
            tab[TILE + i * 8 + u] = jnp.int32(tiles)
            tab[SEAT + i * 8 + u] = zero
        for u in range(4):
            tab[SLOT + i * 4 + u] = zero
        return carry

    lax.fori_loop(0, ROOM // 8, clear, 0)
    for copy in copies[:3]:
        copy.wait()

    def count(i, counts):
        for u in range(4):
            j = slot_ref[i * 4 + u]
            counts = tuple(c + (j == g).astype(jnp.int32) for g, c in enumerate(counts))
        return counts

    counts = lax.fori_loop(0, tiles // 4, count, (zero,) * slots)
    at = zero
    for j in range(slots):
        ray = ray_ref[j]
        owner = ray // own
        o = ray - owner * own
        theirs = owner // CORES
        side = jnp.where(lax.rem(owner, CORES) == core, 0, ny)
        tab[SEND + j] = (side + lax.rem(theirs - y + ny, ny)) * own + o
        tab[TAKE + j] = (side + lax.rem(y - theirs + ny, ny)) * own + o
        ray_ref[j] = at
        pairs = (counts[j] + 1) // 2

        def mark(i, carry, j=j, first=at // 2):
            tab[SLOT + first + i] = jnp.int32(j)
            return carry

        lax.fori_loop(0, pairs, mark, 0)
        at = at + 2 * pairs
    tab[STEPS] = (at + 2 * UNROLL - 1) // (2 * UNROLL)

    def place(i, carry):
        for u in range(4):
            t = i * 4 + u
            b, j = block_ref[t], slot_ref[t]
            seat = ray_ref[j]
            ray_ref[j] = seat + 1
            tab[TILE + seat] = t
            tab[SEAT + seat] = lax.rem(me - lax.rem(b, NX) + NX, NX) * nz + b // NX
        return carry

    lax.fori_loop(0, tiles // 4, place, 0)
    copies[3].wait()


def sweep(tab, body):
    def step(i, carry):
        for u in range(UNROLL):
            pair = i * UNROLL + u
            body(tab[SLOT + pair], *[tab[at + 2 * pair + n] for at in (TILE, SEAT) for n in (0, 1)])
        return carry

    lax.fori_loop(0, tab[STEPS], step, 0)


def forward_kernel(tab, tiles_ref, *refs):
    columns, (mine_ref, other_ref, acc, pix) = refs[:NX], refs[NX:]
    nz, half = columns[0].shape[0], mine_ref.shape[0]
    for d, column in enumerate(columns):
        pix[d * nz : (d + 1) * nz] = column[...]
    acc[...] = jnp.zeros_like(acc)
    for out in (mine_ref, other_ref):
        out[...] = jnp.zeros_like(out)

    def body(j, t, u, p, q):
        pair = jnp.concatenate([tiles_ref[t], tiles_ref[u]], axis=1)
        pixels = jnp.concatenate([pix[p], pix[q]], axis=0)
        acc[j] += jnp.dot(pair, pixels, preferred_element_type=F32)

    sweep(tab, body)
    for j in range(acc.shape[0]):
        seat = tab[SEND + j]

        @pl.when(seat < half)
        def _():
            mine_ref[seat] = acc[j].astype(BF16)

        @pl.when(seat >= half)
        def _():
            other_ref[seat - half] = acc[j].astype(BF16)


def merge_kernel(own, mine_ref, other_ref, near_ref, *far_refs):
    near_ref[...] = mine_ref[:own].astype(F32) + other_ref[:own].astype(F32)
    for d, ref in enumerate(far_refs, 1):
        rows = slice(d * own, (d + 1) * own)
        ref[...] = (mine_ref[rows].astype(F32) + other_ref[rows].astype(F32)).astype(BF16)


def owner_kernel(obs_ref, scale_ref, near_ref, *refs):
    far, (res_ref, flip_ref) = refs[:-2], refs[-2:]
    for o in range(obs_ref.shape[0]):
        total = near_ref[o]
        for ref in far:
            total += ref[o].astype(F32)
        value = scale_ref[o].astype(F32) * (total - obs_ref[o].astype(F32))
        res_ref[o] = value.astype(BF16)
        flip_ref[o] = value.T.astype(BF16)


def backward_kernel(tab, tiles_ref, *refs):
    ins, outs, (acc, rays) = refs[: -1 - 2 * NX], refs[-1 - 2 * NX : -2], refs[-2:]
    own, (nz, _, edge) = ins[0].shape[0], outs[0].shape
    for n, ref in enumerate(ins):
        rays[n * own : (n + 1) * own] = ref[...]
    acc[...] = jnp.zeros_like(acc)

    def body(j, t, u, p, q):
        pair = jnp.concatenate([tiles_ref[t], tiles_ref[u]], axis=1)
        terms = jnp.dot(rays[tab[TAKE + j]], pair, preferred_element_type=F32)
        acc[p] += terms[:, :edge]
        acc[q] += terms[:, edge:]

    sweep(tab, body)
    outs[0][...] = acc[:nz].astype(BF16)
    for n, out in enumerate(outs[1:]):
        at = (NX - 1 - n // 2) * nz + n % 2 * (nz // 2)
        out[...] = acc[at : at + nz // 2].astype(BF16)


def add_kernel(*refs):
    for n in range(len(refs) // 3):
        refs[-2 + n][...] = (refs[2 * n][...].astype(F32) + refs[2 * n + 1][...].astype(F32)).astype(BF16)


def sum_kernel(here_ref, *refs):
    out, half = refs[-1], here_ref.shape[0] // 2
    for n in range(2):
        rows = slice(n * half, (n + 1) * half)
        total = here_ref[rows].astype(F32)
        for ref in refs[2 * n : 2 * n + 2]:
            total += ref[...].astype(F32)
        out[rows] = total.astype(BF16)


def update_kernel(step_size, grad_ref, cur_ref, new_ref, *copies):
    total = grad_ref[0].astype(F32)
    for k in range(1, grad_ref.shape[0]):
        total += grad_ref[k].astype(F32)
    new = jnp.maximum(cur_ref[...] - step_size * total.T, 0.0)
    new_ref[...] = new
    for copy in copies:
        value = new.astype(BF16)
        for k in range(copy.shape[0]):
            copy[k] = value


def call(kernel, shapes, specs, mib, scratch=(), outs=None, work=0):
    return pl.pallas_call(
        kernel,
        out_shape=tuple(jax.ShapeDtypeStruct(shape, dtype) for shape, dtype in shapes),
        in_specs=specs,
        out_specs=outs or (VMEM,) * len(shapes),
        scratch_shapes=list(scratch),
        compiler_params=pltpu.CompilerParams(vmem_limit_bytes=mib << 20),
        cost_estimate=pl.CostEstimate(flops=work, transcendentals=0, bytes_accessed=2 << 20),
    )


def shards(image, tiles, tile_slot, tile_block, slot_ray, sinogram, weights):
    n_space = lax.axis_size("space")
    n_angle = lax.axis_size("angle")
    nz, ny = n_angle // NX, n_space // CORES
    z_groups = [[z * NX + x for z in range(nz)] for x in range(NX)]
    tile_mats = tiles[0]
    own = sinogram.shape[1]
    edge = tile_mats.shape[1]
    slices = image.shape[1]
    blocks = image.shape[0] * n_angle // edge
    slots = slot_ray.shape[1]
    count = tile_slot.shape[1]
    step_size = 0.2 * math.sqrt(blocks / (n_angle * own))
    tile = (edge, slices)
    work = 2 * edge * edge * slices * count

    def along_x(value, d):
        return lax.ppermute(value, "angle", [(i, i // NX * NX + (i + d) % NX) for i in range(n_angle)])

    def along_y(value, d):
        return lax.ppermute(value, "space", [(i, (i + d * CORES) % n_space) for i in range(n_space)])

    def across(value):
        return lax.ppermute(value, "space", [(i, i ^ 1) for i in range(n_space)])

    def along_z(value):
        return lax.all_to_all(value, "angle", 0, 0, axis_index_groups=z_groups, tiled=True)

    def iterate(iteration, current, copies, table):
        column = along_z(copies)
        if table is None:
            sources = (tile_slot[0], tile_block[0], slot_ray[0], tile_mats)
            table = call(
                functools.partial(table_kernel, own, ny, nz),
                [((TABLE,), jnp.int32), ((count + 1, *tile_mats.shape[1:]), BF16)],
                [HBM] * 4,
                8,
                [pltpu.SMEM((size,), jnp.int32) for size in (count, count, slots)]
                + [pltpu.SemaphoreType.DMA((4,))],
                outs=(SMEM, VMEM),
                work=work,
            )(*[pltpu.with_memory_space_constraint(source, pltpu.HBM) for source in sources])
        columns = {d: along_x(column, d) for d in (RIGHT, LEFT, ACROSS)}
        columns[0] = column
        mine, other = call(
            forward_kernel,
            [((ny * own, *tile), BF16)] * 2,
            [SMEM] + [VMEM] * (1 + NX),
            12,
            [pltpu.VMEM((slots, *tile), F32), pltpu.VMEM((blocks, *tile), BF16)],
            work=work,
        )(*table, *[columns[d] for d in range(NX)])
        near, *far = call(
            functools.partial(merge_kernel, own),
            [((own, *tile), F32)] + [((own, *tile), BF16)] * (ny - 1),
            [VMEM] * 2,
            8,
        )(mine, across(other))
        residual, flipped = call(
            owner_kernel, [((own, *tile), BF16)] * 2, [VMEM] * (2 + ny), 8
        )(sinogram[0], weights[0], near, *[along_y(far[d - 1], d) for d in range(1, ny)])
        same = [flipped] + [along_y(flipped, d) for d in range(1, ny)]
        rays = same + [across(value) for value in same]

        half = ((nz // 2, *tile), BF16)
        here, right_low, right_high, far_low, far_high, left_low, left_high = call(
            backward_kernel,
            [((nz, *tile), BF16)] + [half] * (2 * NX - 2),
            [SMEM] + [VMEM] * (1 + len(rays)),
            12,
            [pltpu.VMEM((blocks, *tile), F32), pltpu.VMEM((n_space * own, *tile), BF16)],
            work=work,
        )(*table, *rays)
        from_left, from_right = along_x(far_low, RIGHT), along_x(far_high, LEFT)
        right_high, left_low = along_x(right_high, RIGHT), along_x(left_low, LEFT)
        right_low, left_high = call(add_kernel, [half] * 2, [VMEM] * 4, 8)(right_low, from_left, left_high, from_right)
        right_low, left_high = along_x(right_low, RIGHT), along_x(left_high, LEFT)
        (column,) = call(sum_kernel, [((nz, *tile), BF16)], [VMEM] * 5, 8)(
            here, right_low, left_low, right_high, left_high
        )
        terms = along_z(column)
        more = iteration + 1 < ITERS
        current, *rest = call(
            functools.partial(update_kernel, step_size), [(tile, F32)] + [((nz, *tile), BF16)] * more, [VMEM] * 2, 8
        )(terms, current)
        return (current, residual, rest[0] if more else None, table)

    current, table = image, None
    copies = jnp.broadcast_to(image.astype(BF16)[None], (nz, *tile))
    for iteration in range(ITERS):
        current, residual, copies, table = iterate(iteration, current, copies, table)
    return (current, residual[None])


def solution(mesh):
    placed = (
        P(("space", "angle"), None),
        P("space", "angle", None, None),
        P("space", "angle"),
        P("space", "angle"),
        P("space", "angle"),
        P("angle", "space", None, None),
        P("angle", "space", None, None),
    )
    return jax.shard_map(
        shards,
        mesh=mesh,
        in_specs=placed,
        out_specs=(P(("space", "angle"), None), P("angle", "space", None, None)),
        check_vma=False,
    )
```

time: 195 us -> 182 us (0.933)
  the two profiles are of different devices: /device:TPU:1 before, /device:TPU:8 now
where the time goes in v3:
time: 182 us; the launch traced here: 178 us
  blocking collectives  59.2 us (33%)
  waiting for transfers between devices  53.3 us (29%)
  starting transfers between devices  48.3 us (27%)
  Pallas kernels  15.8 us (9%)
    all_to_all x4, blocking collectives, along_z(): lax.all_to_all(value, 'angle', 0, 0, axis_index_groups=z_groups, tiled=True)  59.2 us
    ppermute x18, starting transfers between devices, along_x(): lax.ppermute(value, 'angle', [(i, i // NX * NX + (i + d) % NX) for i in r...  27.9 us
    ppermute x18, waiting for transfers between devices, along_x(): lax.ppermute(value, 'angle', [(i, i // NX * NX + (i + d) % NX) for i in r...  26 us
    ppermute x12, waiting for transfers between devices, along_y(): lax.ppermute(value, 'space', [(i, (i + d * CORES) % n_space) for i in ran...  20.9 us
    ppermute x12, starting transfers between devices, along_y(): lax.ppermute(value, 'space', [(i, (i + d * CORES) % n_space) for i in ran...  19.7 us
    ppermute x10, waiting for transfers between devices, across(): return lax.ppermute(value, 'space', [(i, i ^ 1) for i in range(n_space)])  6.47 us
    pallas_call x2, Pallas kernels, iterate(): call(forward_kernel, [((ny * own, *tile), BF16)] * 2, [SMEM] + [VMEM] * (...  4.49 us
    pallas_call x2, Pallas kernels, iterate(): call(backward_kernel, [((nz, *tile), BF16)] + [half] * (2 * NX - 2), [SME...  4.43 us
  transfers between devices with their start and end apart: 40, of which 29 were waited for; matrix products, arithmetic and copies ran while one was open for 0% of the time, Pallas kernels for 2%

profile of v3, /device:TPU:8, one launch (start us, length us, event | category | flops | bytes accessed | tf_op | source)
XLA Modules:
  0.0 178.3 jit_solution(5260142718776888317)
XLA Ops:
  1.5 20.1 %all_to_all.20.refs_0_ = bf16[8,128,128]{2,1,0:T(8,128)(2,1)S(1)} all-to-all(bf16[8,128,128]{2,1,0:T(8,128)(2,1)S(1)} %broadcast_in_dim.4), channel_id=1, replica_groups={{0,4,8,12,16,20,24,28},{1,5,9,13,17,21,25,29},{2,6,10,14,18,22,26,30},{..., dimensions={0} | all-to-all | bytes 524288 | tf_op jit(solution)/shard_map/all_to_all | solution.py:234
  21.7 2.8 %collective-permute-start.2 = (bf16[8,128,128]{2,1,0:T(8,128)(2,1)S(1)}, bf16[8,128,128]{2,1,0:T(8,128)(2,1)S(1)}, u32[]{:S(2)}, u32[]{:S(2)}) collective-permute-start(bf16[8,128,128]{2,1,0:T(8,128)(2,1)S(1)} %all_to_all.20.refs_0_), channel_id=1, source_target_pairs={{0,3},{1,0},{2,1},{3,2},{4,7},{5,4},{6,5},{7,6},{8,11},{9,8},{10,9... | collective-permute-start | bytes 786440 | tf_op jit(solution)/shard_map/ppermute | solution.py:225
  26.1 3.9 %shard_map.86 = (s32[384]{0:T(512)S(1)}, bf16[97,128,128]{2,1,0:T(8,128)(2,1)S(1)}) custom-call(s32[96]{0:T(128)} %bitcast.12, s32[96]{0:T(128)} %bitcast.13, s32[8]{0:T(128)} %bitcast.14, bf16[96,128,128]{2,1,0:T(8,128)(2,1)} %bitcast.11), custom_call_target="tpu_custom_call" | custom-call | flops 402653184 | bytes 2097152 | tf_op jit(solution)/shard_map/pallas_call | solution.py:240
  30.1 3.9 %collective-permute-done.2.refs_3_ = bf16[8,128,128]{2,1,0:T(8,128)(2,1)S(1)} collective-permute-done((bf16[8,128,128]{2,1,0:T(8,128)(2,1)S(1)}, bf16[8,128,128]{2,1,0:T(8,128)(2,1)S(1)}, u32[]{:S(2)}, u32[]{:S(2)}) %collective-permute-start.2) | collective-permute-done | bytes 262176 | tf_op jit(solution)/shard_map/ppermute | solution.py:225
  34.9 2.8 %collective-permute-done.refs_1_ = bf16[8,128,128]{2,1,0:T(8,128)(2,1)S(1)} collective-permute-done((bf16[8,128,128]{2,1,0:T(8,128)(2,1)S(1)}, bf16[8,128,128]{2,1,0:T(8,128)(2,1)S(1)}, u32[]{:S(2)}, u32[]{:S(2)}) %collective-permute-start) | collective-permute-done | bytes 262176 | tf_op jit(solution)/shard_map/ppermute | solution.py:225
  37.6 2.2 %shard_map.87 = (bf16[16,128,128]{2,1,0:T(8,128)(2,1)S(1)}, bf16[16,128,128]{2,1,0:T(8,128)(2,1)S(1)}) custom-call(s32[384]{0:T(512)S(1)} %get-tuple-element.39.tab, bf16[97,128,128]{2,1,0:T(8,128)(2,1)S(1)} %get-tuple-element.40.tiles_ref, bf16[8,128,128]{2,1,0:T(8,128)(2,1)S(1)} %all_to_all.20.refs_0_, ...), custom_call_target="tpu_custom_call" | custom-call | flops 402653184 | bytes 2097152 | tf_op jit(solution)/shard_map/pallas_call | solution.py:252
  44.6 2.4 %collective-permute-start.6 = (bf16[4,128,128]{2,1,0:T(8,128)(2,1)S(1)}, bf16[4,128,128]{2,1,0:T(8,128)(2,1)S(1)}, u32[]{:S(2)}, u32[]{:S(2)}) collective-permute-start(bf16[4,128,128]{2,1,0:T(8,128)(2,1)S(1)} %get-tuple-element.46), channel_id=1, source_target_pairs={{0,192},{32,224},{64,0},{96,32},{128,64},{160,96},{192,128},{224,1... | collective-permute-start | bytes 393224 | tf_op jit(solution)/shard_map/ppermute | solution.py:228
  47.8 3.7 %collective-permute-done.5.refs_1_ = bf16[4,128,128]{2,1,0:T(8,128)(2,1)S(1)} collective-permute-done((bf16[4,128,128]{2,1,0:T(8,128)(2,1)S(1)}, bf16[4,128,128]{2,1,0:T(8,128)(2,1)S(1)}, u32[]{:S(2)}, u32[]{:S(2)}) %collective-permute-start.5) | collective-permute-done | bytes 131104 | tf_op jit(solution)/shard_map/ppermute | solution.py:228
  54.1 2.0 %collective-permute-start.8 = (bf16[4,128,128]{2,1,0:T(8,128)(2,1)S(1)}, bf16[4,128,128]{2,1,0:T(8,128)(2,1)S(1)}, u32[]{:S(2)}, u32[]{:S(2)}) collective-permute-start(bf16[4,128,128]{2,1,0:T(8,128)(2,1)S(1)} %get-tuple-element.47.refs_0_), channel_id=1, source_target_pairs={{0,128},{32,160},{64,192},{96,224},{128,0},{160,32},{192,64},{224,... | collective-permute-start | bytes 393224 | tf_op jit(solution)/shard_map/ppermute | solution.py:228
  57.7 2.0 %collective-permute-done.9.refs_3_ = bf16[4,128,128]{2,1,0:T(8,128)(2,1)S(1)} collective-permute-done((bf16[4,128,128]{2,1,0:T(8,128)(2,1)S(1)}, bf16[4,128,128]{2,1,0:T(8,128)(2,1)S(1)}, u32[]{:S(2)}, u32[]{:S(2)}) %collective-permute-start.9) | collective-permute-done | bytes 131104 | tf_op jit(solution)/shard_map/ppermute | solution.py:228
  64.0 2.2 %shard_map.90 = (bf16[8,128,128]{2,1,0:T(8,128)(2,1)S(1)}, bf16[4,128,128]{2,1,0:T(8,128)(2,1)S(1)}, bf16[4,128,128]{2,1,0:T(8,128)(2,1)S(1)}, bf16[4,128,128]{2...) custom-call(s32[384]{0:T(512)S(1)} %get-tuple-element.39.tab, ...), custom_call_target="tpu_custom_call" | custom-call | flops 402653184 | bytes 2097152 | tf_op jit(solution)/shard_map/pallas_call | solution.py:273
  66.5 3.2 %collective-permute-start.15 = (bf16[4,128,128]{2,1,0:T(8,128)(2,1)S(1)}, bf16[4,128,128]{2,1,0:T(8,128)(2,1)S(1)}, u32[]{:S(2)}, u32[]{:S(2)}) collective-permute-start(bf16[4,128,128]{2,1,0:T(8,128)(2,1)S(1)} %get-tuple-element.52), channel_id=1, source_target_pairs={{0,3},{1,0},{2,1},{3,2},{4,7},{5,4},{6,5},{7,6},{8,11},{9,8},{10,9... | collective-permute-start | bytes 393224 | tf_op jit(solution)/shard_map/ppermute | solution.py:225
  69.7 2.0 %collective-permute-start.18 = (bf16[4,128,128]{2,1,0:T(8,128)(2,1)S(1)}, bf16[4,128,128]{2,1,0:T(8,128)(2,1)S(1)}, u32[]{:S(2)}, u32[]{:S(2)}) collective-permute-start(bf16[4,128,128]{2,1,0:T(8,128)(2,1)S(1)} %get-tuple-element.55), channel_id=1, source_target_pairs={{0,1},{1,2},{2,3},{3,0},{4,5},{5,6},{6,7},{7,4},{8,9},{9,10},{10,1... | collective-permute-start | bytes 393224 | tf_op jit(solution)/shard_map/ppermute | solution.py:225
  73.8 3.8 %collective-permute-start.19 = (bf16[4,128,128]{2,1,0:T(8,128)(2,1)S(1)}, bf16[4,128,128]{2,1,0:T(8,128)(2,1)S(1)}, u32[]{:S(2)}, u32[]{:S(2)}) collective-permute-start(bf16[4,128,128]{2,1,0:T(8,128)(2,1)S(1)} %get-tuple-element.56), channel_id=1, source_target_pairs={{0,3},{1,0},{2,1},{3,2},{4,7},{5,4},{6,5},{7,6},{8,11},{9,8},{10,9... | collective-permute-start | bytes 393224 | tf_op jit(solution)/shard_map/ppermute | solution.py:225
  77.5 2.9 %collective-permute-done.16.refs_0_ = bf16[4,128,128]{2,1,0:T(8,128)(2,1)S(1)} collective-permute-done((bf16[4,128,128]{2,1,0:T(8,128)(2,1)S(1)}, bf16[4,128,128]{2,1,0:T(8,128)(2,1)S(1)}, u32[]{:S(2)}, u32[]{:S(2)}) %collective-permute-start.16) | collective-permute-done | bytes 131104 | tf_op jit(solution)/shard_map/ppermute | solution.py:225
  80.5 13.3 %all_to_all.21.grad_ref = bf16[8,128,128]{2,1,0:T(8,128)(2,1)S(1)} all-to-all(bf16[8,128,128]{2,1,0:T(8,128)(2,1)S(1)} %shard_map.92), channel_id=1, replica_groups={{0,4,8,12,16,20,24,28},{1,5,9,13,17,21,25,29},{2,6,10,14,18,22,26,30},{..., dimensions={0} | all-to-all | bytes 524288 | tf_op jit(solution)/shard_map/all_to_all | solution.py:234
  93.9 12.9 %all_to_all.22.refs_0_ = bf16[8,128,128]{2,1,0:T(8,128)(2,1)S(1)} all-to-all(bf16[8,128,128]{2,1,0:T(8,128)(2,1)S(1)} %get-tuple-element.57), channel_id=1, replica_groups={{0,4,8,12,16,20,24,28},{1,5,9,13,17,21,25,29},{2,6,10,14,18,22,26,30},{..., dimensions={0} | all-to-all | bytes 524288 | tf_op jit(solution)/shard_map/all_to_all | solution.py:234
  106.8 3.3 %collective-permute-start.22 = (bf16[8,128,128]{2,1,0:T(8,128)(2,1)S(1)}, bf16[8,128,128]{2,1,0:T(8,128)(2,1)S(1)}, u32[]{:S(2)}, u32[]{:S(2)}) collective-permute-start(bf16[8,128,128]{2,1,0:T(8,128)(2,1)S(1)} %all_to_all.22.refs_0_), channel_id=1, source_target_pairs={{0,3},{1,0},{2,1},{3,2},{4,7},{5,4},{6,5},{7,6},{8,11},{9,8},{10,9... | collective-permute-start | bytes 786440 | tf_op jit(solution)/shard_map/ppermute | solution.py:225
  111.7 5.1 %collective-permute-done.22.refs_3_ = bf16[8,128,128]{2,1,0:T(8,128)(2,1)S(1)} collective-permute-done((bf16[8,128,128]{2,1,0:T(8,128)(2,1)S(1)}, bf16[8,128,128]{2,1,0:T(8,128)(2,1)S(1)}, u32[]{:S(2)}, u32[]{:S(2)}) %collective-permute-start.22) | collective-permute-done | bytes 262176 | tf_op jit(solution)/shard_map/ppermute | solution.py:225
  118.0 2.6 %collective-permute-done.20.refs_1_ = bf16[8,128,128]{2,1,0:T(8,128)(2,1)S(1)} collective-permute-done((bf16[8,128,128]{2,1,0:T(8,128)(2,1)S(1)}, bf16[8,128,128]{2,1,0:T(8,128)(2,1)S(1)}, u32[]{:S(2)}, u32[]{:S(2)}) %collective-permute-start.20) | collective-permute-done | bytes 262176 | tf_op jit(solution)/shard_map/ppermute | solution.py:225
  120.6 2.2 %shard_map.94 = (bf16[16,128,128]{2,1,0:T(8,128)(2,1)S(1)}, bf16[16,128,128]{2,1,0:T(8,128)(2,1)S(1)}) custom-call(s32[384]{0:T(512)S(1)} %get-tuple-element.39.tab, bf16[97,128,128]{2,1,0:T(8,128)(2,1)S(1)} %get-tuple-element.40.tiles_ref, bf16[8,128,128]{2,1,0:T(8,128)(2,1)S(1)} %all_to_all.22.refs_0_, ...), custom_call_target="tpu_custom_call" | custom-call | flops 402653184 | bytes 2097152 | tf_op jit(solution)/shard_map/pallas_call | solution.py:252
  126.5 3.1 %collective-permute-start.25 = (bf16[4,128,128]{2,1,0:T(8,128)(2,1)S(1)}, bf16[4,128,128]{2,1,0:T(8,128)(2,1)S(1)}, u32[]{:S(2)}, u32[]{:S(2)}) collective-permute-start(bf16[4,128,128]{2,1,0:T(8,128)(2,1)S(1)} %get-tuple-element.62), channel_id=1, source_target_pairs={{0,128},{32,160},{64,192},{96,224},{128,0},{160,32},{192,64},{224,... | collective-permute-start | bytes 393224 | tf_op jit(solution)/shard_map/ppermute | solution.py:228
  129.7 2.3 %collective-permute-done.24.refs_0_ = bf16[4,128,128]{2,1,0:T(8,128)(2,1)S(1)} collective-permute-done((bf16[4,128,128]{2,1,0:T(8,128)(2,1)S(1)}, bf16[4,128,128]{2,1,0:T(8,128)(2,1)S(1)}, u32[]{:S(2)}, u32[]{:S(2)}) %collective-permute-start.24) | collective-permute-done | bytes 131104 | tf_op jit(solution)/shard_map/ppermute | solution.py:228
  132.0 2.5 %collective-permute-done.25.refs_1_ = bf16[4,128,128]{2,1,0:T(8,128)(2,1)S(1)} collective-permute-done((bf16[4,128,128]{2,1,0:T(8,128)(2,1)S(1)}, bf16[4,128,128]{2,1,0:T(8,128)(2,1)S(1)}, u32[]{:S(2)}, u32[]{:S(2)}) %collective-permute-start.25) | collective-permute-done | bytes 131104 | tf_op jit(solution)/shard_map/ppermute | solution.py:228
  139.8 2.6 %collective-permute-start.27 = (bf16[4,128,128]{2,1,0:T(8,128)(2,1)S(1)}, bf16[4,128,128]{2,1,0:T(8,128)(2,1)S(1)}, u32[]{:S(2)}, u32[]{:S(2)}) collective-permute-start(bf16[4,128,128]{2,1,0:T(8,128)(2,1)S(1)} %get-tuple-element.64.refs_0_), channel_id=1, source_target_pairs={{0,64},{32,96},{64,128},{96,160},{128,192},{160,224},{192,0},{224,... | collective-permute-start | bytes 393224 | tf_op jit(solution)/shard_map/ppermute | solution.py:228
  143.0 3.1 %collective-permute-done.28.refs_2_ = bf16[4,128,128]{2,1,0:T(8,128)(2,1)S(1)} collective-permute-done((bf16[4,128,128]{2,1,0:T(8,128)(2,1)S(1)}, bf16[4,128,128]{2,1,0:T(8,128)(2,1)S(1)}, u32[]{:S(2)}, u32[]{:S(2)}) %collective-permute-start.28) | collective-permute-done | bytes 131104 | tf_op jit(solution)/shard_map/ppermute | solution.py:228
  148.4 2.2 %shard_map.97 = (bf16[8,128,128]{2,1,0:T(8,128)(2,1)S(1)}, bf16[4,128,128]{2,1,0:T(8,128)(2,1)S(1)}, bf16[4,128,128]{2,1,0:T(8,128)(2,1)S(1)}, bf16[4,128,128]{2...) custom-call(s32[384]{0:T(512)S(1)} %get-tuple-element.39.tab, ...), custom_call_target="tpu_custom_call" | custom-call | flops 402653184 | bytes 2097152 | tf_op jit(solution)/shard_map/pallas_call | solution.py:273
  150.7 3.2 %collective-permute-start.35 = (bf16[4,128,128]{2,1,0:T(8,128)(2,1)S(1)}, bf16[4,128,128]{2,1,0:T(8,128)(2,1)S(1)}, u32[]{:S(2)}, u32[]{:S(2)}) collective-permute-start(bf16[4,128,128]{2,1,0:T(8,128)(2,1)S(1)} %get-tuple-element.69), channel_id=1, source_target_pairs={{0,3},{1,0},{2,1},{3,2},{4,7},{5,4},{6,5},{7,6},{8,11},{9,8},{10,9... | collective-permute-start | bytes 393224 | tf_op jit(solution)/shard_map/ppermute | solution.py:225
  153.9 2.0 %collective-permute-start.38 = (bf16[4,128,128]{2,1,0:T(8,128)(2,1)S(1)}, bf16[4,128,128]{2,1,0:T(8,128)(2,1)S(1)}, u32[]{:S(2)}, u32[]{:S(2)}) collective-permute-start(bf16[4,128,128]{2,1,0:T(8,128)(2,1)S(1)} %get-tuple-element.72), channel_id=1, source_target_pairs={{0,1},{1,2},{2,3},{3,0},{4,5},{5,6},{6,7},{7,4},{8,9},{9,10},{10,1... | collective-permute-start | bytes 393224 | tf_op jit(solution)/shard_map/ppermute | solution.py:225
  157.9 3.8 %collective-permute-start.39 = (bf16[4,128,128]{2,1,0:T(8,128)(2,1)S(1)}, bf16[4,128,128]{2,1,0:T(8,128)(2,1)S(1)}, u32[]{:S(2)}, u32[]{:S(2)}) collective-permute-start(bf16[4,128,128]{2,1,0:T(8,128)(2,1)S(1)} %get-tuple-element.73), channel_id=1, source_target_pairs={{0,3},{1,0},{2,1},{3,2},{4,7},{5,4},{6,5},{7,6},{8,11},{9,8},{10,9... | collective-permute-start | bytes 393224 | tf_op jit(solution)/shard_map/ppermute | solution.py:225
  161.7 2.9 %collective-permute-done.36.refs_0_ = bf16[4,128,128]{2,1,0:T(8,128)(2,1)S(1)} collective-permute-done((bf16[4,128,128]{2,1,0:T(8,128)(2,1)S(1)}, bf16[4,128,128]{2,1,0:T(8,128)(2,1)S(1)}, u32[]{:S(2)}, u32[]{:S(2)}) %collective-permute-start.36) | collective-permute-done | bytes 131104 | tf_op jit(solution)/shard_map/ppermute | solution.py:225
  164.7 12.9 %all_to_all.23.grad_ref = bf16[8,128,128]{2,1,0:T(8,128)(2,1)S(1)} all-to-all(bf16[8,128,128]{2,1,0:T(8,128)(2,1)S(1)} %shard_map.99), channel_id=1, replica_groups={{0,4,8,12,16,20,24,28},{1,5,9,13,17,21,25,29},{2,6,10,14,18,22,26,30},{..., dimensions={0} | all-to-all | bytes 524288 | tf_op jit(solution)/shard_map/all_to_all | solution.py:234
  (75 shorter events, 37.6 us)
Async XLA Ops:
  21.7 12.3 %collective-permute-start.2 = (bf16[8,128,128]{2,1,0:T(8,128)(2,1)S(1)}, bf16[8,128,128]{2,1,0:T(8,128)(2,1)S(1)}, u32[]{:S(2)}, u32[]{:S(2)}) collective-permute-start(bf16[8,128,128]{2,1,0:T(8,128)(2,1)S(1)} %all_to_all.20.refs_0_), channel_id=1, source_target_pairs={{0,3},{1,0},{2,1},{3,2},{4,7},{5,4},{6,5},{7,6},{8,11},{9,8},{10,9... | collective-permute-start | bytes 786440 | tf_op jit(solution)/shard_map/ppermute | solution.py:225
  24.4 10.5 %collective-permute-start.1 = (bf16[8,128,128]{2,1,0:T(8,128)(2,1)S(1)}, bf16[8,128,128]{2,1,0:T(8,128)(2,1)S(1)}, u32[]{:S(2)}, u32[]{:S(2)}) collective-permute-start(bf16[8,128,128]{2,1,0:T(8,128)(2,1)S(1)} %all_to_all.20.refs_0_), channel_id=1, source_target_pairs={{0,2},{1,3},{2,0},{3,1},{4,6},{5,7},{6,4},{7,5},{8,10},{9,11},{10,... | collective-permute-start | bytes 786440 | tf_op jit(solution)/shard_map/ppermute | solution.py:225
  25.2 12.4 %collective-permute-start = (bf16[8,128,128]{2,1,0:T(8,128)(2,1)S(1)}, bf16[8,128,128]{2,1,0:T(8,128)(2,1)S(1)}, u32[]{:S(2)}, u32[]{:S(2)}) collective-permute-start(bf16[8,128,128]{2,1,0:T(8,128)(2,1)S(1)} %all_to_all.20.refs_0_), channel_id=1, source_target_pairs={{0,1},{1,2},{2,3},{3,0},{4,5},{5,6},{6,7},{7,4},{8,9},{9,10},{10,1... | collective-permute-start | bytes 786440 | tf_op jit(solution)/shard_map/ppermute | solution.py:225
  42.0 5.8 %collective-permute-start.4 = (bf16[4,128,128]{2,1,0:T(8,128)(2,1)S(1)}, bf16[4,128,128]{2,1,0:T(8,128)(2,1)S(1)}, u32[]{:S(2)}, u32[]{:S(2)}) collective-permute-start(bf16[4,128,128]{2,1,0:T(8,128)(2,1)S(1)} %get-tuple-element.44), channel_id=1, source_target_pairs={{0,64},{32,96},{64,128},{96,160},{128,192},{160,224},{192,0},{224,... | collective-permute-start | bytes 393224 | tf_op jit(solution)/shard_map/ppermute | solution.py:228
  43.7 7.9 %collective-permute-start.5 = (bf16[4,128,128]{2,1,0:T(8,128)(2,1)S(1)}, bf16[4,128,128]{2,1,0:T(8,128)(2,1)S(1)}, u32[]{:S(2)}, u32[]{:S(2)}) collective-permute-start(bf16[4,128,128]{2,1,0:T(8,128)(2,1)S(1)} %get-tuple-element.45), channel_id=1, source_target_pairs={{0,128},{32,160},{64,192},{96,224},{128,0},{160,32},{192,64},{224,... | collective-permute-start | bytes 393224 | tf_op jit(solution)/shard_map/ppermute | solution.py:228
  44.6 7.9 %collective-permute-start.6 = (bf16[4,128,128]{2,1,0:T(8,128)(2,1)S(1)}, bf16[4,128,128]{2,1,0:T(8,128)(2,1)S(1)}, u32[]{:S(2)}, u32[]{:S(2)}) collective-permute-start(bf16[4,128,128]{2,1,0:T(8,128)(2,1)S(1)} %get-tuple-element.46), channel_id=1, source_target_pairs={{0,192},{32,224},{64,0},{96,32},{128,64},{160,96},{192,128},{224,1... | collective-permute-start | bytes 393224 | tf_op jit(solution)/shard_map/ppermute | solution.py:228
  53.3 6.4 %collective-permute-start.9 = (bf16[4,128,128]{2,1,0:T(8,128)(2,1)S(1)}, bf16[4,128,128]{2,1,0:T(8,128)(2,1)S(1)}, u32[]{:S(2)}, u32[]{:S(2)}) collective-permute-start(bf16[4,128,128]{2,1,0:T(8,128)(2,1)S(1)} %get-tuple-element.47.refs_0_), channel_id=1, source_target_pairs={{0,192},{32,224},{64,0},{96,32},{128,64},{160,96},{192,128},{224,1... | collective-permute-start | bytes 393224 | tf_op jit(solution)/shard_map/ppermute | solution.py:228
  54.1 7.3 %collective-permute-start.8 = (bf16[4,128,128]{2,1,0:T(8,128)(2,1)S(1)}, bf16[4,128,128]{2,1,0:T(8,128)(2,1)S(1)}, u32[]{:S(2)}, u32[]{:S(2)}) collective-permute-start(bf16[4,128,128]{2,1,0:T(8,128)(2,1)S(1)} %get-tuple-element.47.refs_0_), channel_id=1, source_target_pairs={{0,128},{32,160},{64,192},{96,224},{128,0},{160,32},{192,64},{224,... | collective-permute-start | bytes 393224 | tf_op jit(solution)/shard_map/ppermute | solution.py:228
  56.1 6.6 %collective-permute-start.7 = (bf16[4,128,128]{2,1,0:T(8,128)(2,1)S(1)}, bf16[4,128,128]{2,1,0:T(8,128)(2,1)S(1)}, u32[]{:S(2)}, u32[]{:S(2)}) collective-permute-start(bf16[4,128,128]{2,1,0:T(8,128)(2,1)S(1)} %get-tuple-element.47.refs_0_), channel_id=1, source_target_pairs={{0,64},{32,96},{64,128},{96,160},{128,192},{160,224},{192,0},{224,... | collective-permute-start | bytes 393224 | tf_op jit(solution)/shard_map/ppermute | solution.py:228
  57.7 4.9 %collective-permute-start.10 = (bf16[4,128,128]{2,1,0:T(8,128)(2,1)S(1)}, bf16[4,128,128]{2,1,0:T(8,128)(2,1)S(1)}, u32[]{:S(2)}, u32[]{:S(2)}) collective-permute-start(bf16[4,128,128]{2,1,0:T(8,128)(2,1)S(1)} %get-tuple-element.47.refs_0_), channel_id=1, source_target_pairs={{0,32},{32,0},{64,96},{96,64},{128,160},{160,128},{192,224},{224,1... | collective-permute-start | bytes 393224 | tf_op jit(solution)/shard_map/ppermute | solution.py:231
  66.2 7.1 %collective-permute-start.14 = (bf16[4,128,128]{2,1,0:T(8,128)(2,1)S(1)}, bf16[4,128,128]{2,1,0:T(8,128)(2,1)S(1)}, u32[]{:S(2)}, u32[]{:S(2)}) collective-permute-start(bf16[4,128,128]{2,1,0:T(8,128)(2,1)S(1)} %get-tuple-element.50), channel_id=1, source_target_pairs={{0,1},{1,2},{2,3},{3,0},{4,5},{5,6},{6,7},{7,4},{8,9},{9,10},{10,1... | collective-permute-start | bytes 393224 | tf_op jit(solution)/shard_map/ppermute | solution.py:225
  66.5 7.1 %collective-permute-start.15 = (bf16[4,128,128]{2,1,0:T(8,128)(2,1)S(1)}, bf16[4,128,128]{2,1,0:T(8,128)(2,1)S(1)}, u32[]{:S(2)}, u32[]{:S(2)}) collective-permute-start(bf16[4,128,128]{2,1,0:T(8,128)(2,1)S(1)} %get-tuple-element.52), channel_id=1, source_target_pairs={{0,3},{1,0},{2,1},{3,2},{4,7},{5,4},{6,5},{7,6},{8,11},{9,8},{10,9... | collective-permute-start | bytes 393224 | tf_op jit(solution)/shard_map/ppermute | solution.py:225
  69.7 7.8 %collective-permute-start.17 = (bf16[4,128,128]{2,1,0:T(8,128)(2,1)S(1)}, bf16[4,128,128]{2,1,0:T(8,128)(2,1)S(1)}, u32[]{:S(2)}, u32[]{:S(2)}) collective-permute-start(bf16[4,128,128]{2,1,0:T(8,128)(2,1)S(1)} %get-tuple-element.54), channel_id=1, source_target_pairs={{0,3},{1,0},{2,1},{3,2},{4,7},{5,4},{6,5},{7,6},{8,11},{9,8},{10,9... | collective-permute-start | bytes 393224 | tf_op jit(solution)/shard_map/ppermute | solution.py:225
  69.7 7.8 %collective-permute-start.18 = (bf16[4,128,128]{2,1,0:T(8,128)(2,1)S(1)}, bf16[4,128,128]{2,1,0:T(8,128)(2,1)S(1)}, u32[]{:S(2)}, u32[]{:S(2)}) collective-permute-start(bf16[4,128,128]{2,1,0:T(8,128)(2,1)S(1)} %get-tuple-element.55), channel_id=1, source_target_pairs={{0,1},{1,2},{2,3},{3,0},{4,5},{5,6},{6,7},{7,4},{8,9},{9,10},{10,1... | collective-permute-start | bytes 393224 | tf_op jit(solution)/shard_map/ppermute | solution.py:225
  73.7 6.7 %collective-permute-start.16 = (bf16[4,128,128]{2,1,0:T(8,128)(2,1)S(1)}, bf16[4,128,128]{2,1,0:T(8,128)(2,1)S(1)}, u32[]{:S(2)}, u32[]{:S(2)}) collective-permute-start(bf16[4,128,128]{2,1,0:T(8,128)(2,1)S(1)} %get-tuple-element.53), channel_id=1, source_target_pairs={{0,1},{1,2},{2,3},{3,0},{4,5},{5,6},{6,7},{7,4},{8,9},{9,10},{10,1... | collective-permute-start | bytes 393224 | tf_op jit(solution)/shard_map/ppermute | solution.py:225
  73.8 6.6 %collective-permute-start.19 = (bf16[4,128,128]{2,1,0:T(8,128)(2,1)S(1)}, bf16[4,128,128]{2,1,0:T(8,128)(2,1)S(1)}, u32[]{:S(2)}, u32[]{:S(2)}) collective-permute-start(bf16[4,128,128]{2,1,0:T(8,128)(2,1)S(1)} %get-tuple-element.56), channel_id=1, source_target_pairs={{0,3},{1,0},{2,1},{3,2},{4,7},{5,4},{6,5},{7,6},{8,11},{9,8},{10,9... | collective-permute-start | bytes 393224 | tf_op jit(solution)/shard_map/ppermute | solution.py:225
  106.8 10.0 %collective-permute-start.22 = (bf16[8,128,128]{2,1,0:T(8,128)(2,1)S(1)}, bf16[8,128,128]{2,1,0:T(8,128)(2,1)S(1)}, u32[]{:S(2)}, u32[]{:S(2)}) collective-permute-start(bf16[8,128,128]{2,1,0:T(8,128)(2,1)S(1)} %all_to_all.22.refs_0_), channel_id=1, source_target_pairs={{0,3},{1,0},{2,1},{3,2},{4,7},{5,4},{6,5},{7,6},{8,11},{9,8},{10,9... | collective-permute-start | bytes 786440 | tf_op jit(solution)/shard_map/ppermute | solution.py:225
  110.1 8.0 %collective-permute-start.21 = (bf16[8,128,128]{2,1,0:T(8,128)(2,1)S(1)}, bf16[8,128,128]{2,1,0:T(8,128)(2,1)S(1)}, u32[]{:S(2)}, u32[]{:S(2)}) collective-permute-start(bf16[8,128,128]{2,1,0:T(8,128)(2,1)S(1)} %all_to_all.22.refs_0_), channel_id=1, source_target_pairs={{0,2},{1,3},{2,0},{3,1},{4,6},{5,7},{6,4},{7,5},{8,10},{9,11},{10,... | collective-permute-start | bytes 786440 | tf_op jit(solution)/shard_map/ppermute | solution.py:225
  110.2 10.4 %collective-permute-start.20 = (bf16[8,128,128]{2,1,0:T(8,128)(2,1)S(1)}, bf16[8,128,128]{2,1,0:T(8,128)(2,1)S(1)}, u32[]{:S(2)}, u32[]{:S(2)}) collective-permute-start(bf16[8,128,128]{2,1,0:T(8,128)(2,1)S(1)} %all_to_all.22.refs_0_), channel_id=1, source_target_pairs={{0,1},{1,2},{2,3},{3,0},{4,5},{5,6},{6,7},{7,4},{8,9},{9,10},{10,1... | collective-permute-start | bytes 786440 | tf_op jit(solution)/shard_map/ppermute | solution.py:225
  125.0 7.0 %collective-permute-start.24 = (bf16[4,128,128]{2,1,0:T(8,128)(2,1)S(1)}, bf16[4,128,128]{2,1,0:T(8,128)(2,1)S(1)}, u32[]{:S(2)}, u32[]{:S(2)}) collective-permute-start(bf16[4,128,128]{2,1,0:T(8,128)(2,1)S(1)} %get-tuple-element.61), channel_id=1, source_target_pairs={{0,64},{32,96},{64,128},{96,160},{128,192},{160,224},{192,0},{224,... | collective-permute-start | bytes 393224 | tf_op jit(solution)/shard_map/ppermute | solution.py:228
  126.5 7.9 %collective-permute-start.25 = (bf16[4,128,128]{2,1,0:T(8,128)(2,1)S(1)}, bf16[4,128,128]{2,1,0:T(8,128)(2,1)S(1)}, u32[]{:S(2)}, u32[]{:S(2)}) collective-permute-start(bf16[4,128,128]{2,1,0:T(8,128)(2,1)S(1)} %get-tuple-element.62), channel_id=1, source_target_pairs={{0,128},{32,160},{64,192},{96,224},{128,0},{160,32},{192,64},{224,... | collective-permute-start | bytes 393224 | tf_op jit(solution)/shard_map/ppermute | solution.py:228
  129.7 6.4 %collective-permute-start.26 = (bf16[4,128,128]{2,1,0:T(8,128)(2,1)S(1)}, bf16[4,128,128]{2,1,0:T(8,128)(2,1)S(1)}, u32[]{:S(2)}, u32[]{:S(2)}) collective-permute-start(bf16[4,128,128]{2,1,0:T(8,128)(2,1)S(1)} %get-tuple-element.63), channel_id=1, source_target_pairs={{0,192},{32,224},{64,0},{96,32},{128,64},{160,96},{192,128},{224,1... | collective-permute-start | bytes 393224 | tf_op jit(solution)/shard_map/ppermute | solution.py:228
  136.9 5.6 %collective-permute-start.29 = (bf16[4,128,128]{2,1,0:T(8,128)(2,1)S(1)}, bf16[4,128,128]{2,1,0:T(8,128)(2,1)S(1)}, u32[]{:S(2)}, u32[]{:S(2)}) collective-permute-start(bf16[4,128,128]{2,1,0:T(8,128)(2,1)S(1)} %get-tuple-element.64.refs_0_), channel_id=1, source_target_pairs={{0,192},{32,224},{64,0},{96,32},{128,64},{160,96},{192,128},{224,1... | collective-permute-start | bytes 393224 | tf_op jit(solution)/shard_map/ppermute | solution.py:228
  138.6 7.6 %collective-permute-start.28 = (bf16[4,128,128]{2,1,0:T(8,128)(2,1)S(1)}, bf16[4,128,128]{2,1,0:T(8,128)(2,1)S(1)}, u32[]{:S(2)}, u32[]{:S(2)}) collective-permute-start(bf16[4,128,128]{2,1,0:T(8,128)(2,1)S(1)} %get-tuple-element.64.refs_0_), channel_id=1, source_target_pairs={{0,128},{32,160},{64,192},{96,224},{128,0},{160,32},{192,64},{224,... | collective-permute-start | bytes 393224 | tf_op jit(solution)/shard_map/ppermute | solution.py:228
  139.8 7.2 %collective-permute-start.27 = (bf16[4,128,128]{2,1,0:T(8,128)(2,1)S(1)}, bf16[4,128,128]{2,1,0:T(8,128)(2,1)S(1)}, u32[]{:S(2)}, u32[]{:S(2)}) collective-permute-start(bf16[4,128,128]{2,1,0:T(8,128)(2,1)S(1)} %get-tuple-element.64.refs_0_), channel_id=1, source_target_pairs={{0,64},{32,96},{64,128},{96,160},{128,192},{160,224},{192,0},{224,... | collective-permute-start | bytes 393224 | tf_op jit(solution)/shard_map/ppermute | solution.py:228
  142.5 4.6 %collective-permute-start.30 = (bf16[4,128,128]{2,1,0:T(8,128)(2,1)S(1)}, bf16[4,128,128]{2,1,0:T(8,128)(2,1)S(1)}, u32[]{:S(2)}, u32[]{:S(2)}) collective-permute-start(bf16[4,128,128]{2,1,0:T(8,128)(2,1)S(1)} %get-tuple-element.64.refs_0_), channel_id=1, source_target_pairs={{0,32},{32,0},{64,96},{96,64},{128,160},{160,128},{192,224},{224,1... | collective-permute-start | bytes 393224 | tf_op jit(solution)/shard_map/ppermute | solution.py:231
  150.6 6.9 %collective-permute-start.34 = (bf16[4,128,128]{2,1,0:T(8,128)(2,1)S(1)}, bf16[4,128,128]{2,1,0:T(8,128)(2,1)S(1)}, u32[]{:S(2)}, u32[]{:S(2)}) collective-permute-start(bf16[4,128,128]{2,1,0:T(8,128)(2,1)S(1)} %get-tuple-element.67), channel_id=1, source_target_pairs={{0,1},{1,2},{2,3},{3,0},{4,5},{5,6},{6,7},{7,4},{8,9},{9,10},{10,1... | collective-permute-start | bytes 393224 | tf_op jit(solution)/shard_map/ppermute | solution.py:225
  150.7 7.1 %collective-permute-start.35 = (bf16[4,128,128]{2,1,0:T(8,128)(2,1)S(1)}, bf16[4,128,128]{2,1,0:T(8,128)(2,1)S(1)}, u32[]{:S(2)}, u32[]{:S(2)}) collective-permute-start(bf16[4,128,128]{2,1,0:T(8,128)(2,1)S(1)} %get-tuple-element.69), channel_id=1, source_target_pairs={{0,3},{1,0},{2,1},{3,2},{4,7},{5,4},{6,5},{7,6},{8,11},{9,8},{10,9... | collective-permute-start | bytes 393224 | tf_op jit(solution)/shard_map/ppermute | solution.py:225
  153.9 7.8 %collective-permute-start.37 = (bf16[4,128,128]{2,1,0:T(8,128)(2,1)S(1)}, bf16[4,128,128]{2,1,0:T(8,128)(2,1)S(1)}, u32[]{:S(2)}, u32[]{:S(2)}) collective-permute-start(bf16[4,128,128]{2,1,0:T(8,128)(2,1)S(1)} %get-tuple-element.71), channel_id=1, source_target_pairs={{0,3},{1,0},{2,1},{3,2},{4,7},{5,4},{6,5},{7,6},{8,11},{9,8},{10,9... | collective-permute-start | bytes 393224 | tf_op jit(solution)/shard_map/ppermute | solution.py:225
  153.9 7.8 %collective-permute-start.38 = (bf16[4,128,128]{2,1,0:T(8,128)(2,1)S(1)}, bf16[4,128,128]{2,1,0:T(8,128)(2,1)S(1)}, u32[]{:S(2)}, u32[]{:S(2)}) collective-permute-start(bf16[4,128,128]{2,1,0:T(8,128)(2,1)S(1)} %get-tuple-element.72), channel_id=1, source_target_pairs={{0,1},{1,2},{2,3},{3,0},{4,5},{5,6},{6,7},{7,4},{8,9},{9,10},{10,1... | collective-permute-start | bytes 393224 | tf_op jit(solution)/shard_map/ppermute | solution.py:225
  157.8 6.7 %collective-permute-start.36 = (bf16[4,128,128]{2,1,0:T(8,128)(2,1)S(1)}, bf16[4,128,128]{2,1,0:T(8,128)(2,1)S(1)}, u32[]{:S(2)}, u32[]{:S(2)}) collective-permute-start(bf16[4,128,128]{2,1,0:T(8,128)(2,1)S(1)} %get-tuple-element.70), channel_id=1, source_target_pairs={{0,1},{1,2},{2,3},{3,0},{4,5},{5,6},{6,7},{7,4},{8,9},{9,10},{10,1... | collective-permute-start | bytes 393224 | tf_op jit(solution)/shard_map/ppermute | solution.py:225
  157.9 6.6 %collective-permute-start.39 = (bf16[4,128,128]{2,1,0:T(8,128)(2,1)S(1)}, bf16[4,128,128]{2,1,0:T(8,128)(2,1)S(1)}, u32[]{:S(2)}, u32[]{:S(2)}) collective-permute-start(bf16[4,128,128]{2,1,0:T(8,128)(2,1)S(1)} %get-tuple-element.73), channel_id=1, source_target_pairs={{0,3},{1,0},{2,1},{3,2},{4,7},{5,4},{6,5},{7,6},{8,11},{9,8},{10,9... | collective-permute-start | bytes 393224 | tf_op jit(solution)/shard_map/ppermute | solution.py:225
  (11 other events, 102.3 us)

commit v4 on v3

--- a/solution.py
+++ b/solution.py
@@ -135,22 +135,25 @@
         ref[...] = (mine_ref[rows].astype(F32) + other_ref[rows].astype(F32)).astype(BF16)
 
 
-def owner_kernel(obs_ref, scale_ref, near_ref, *refs):
-    far, (res_ref, flip_ref) = refs[:-2], refs[-2:]
+def owner_kernel(far_count, obs_ref, scale_ref, near_ref, *refs):
+    far, flip_ref, res = refs[: far_count], refs[far_count], refs[far_count + 1 :]
     for o in range(obs_ref.shape[0]):
         total = near_ref[o]
         for ref in far:
             total += ref[o].astype(F32)
         value = scale_ref[o].astype(F32) * (total - obs_ref[o].astype(F32))
-        res_ref[o] = value.astype(BF16)
+        for ref in res:
+            ref[o] = value.astype(BF16)
         flip_ref[o] = value.T.astype(BF16)
 
 
 def backward_kernel(tab, tiles_ref, *refs):
     ins, outs, (acc, rays) = refs[: -1 - 2 * NX], refs[-1 - 2 * NX : -2], refs[-2:]
-    own, (nz, _, edge) = ins[0].shape[0], outs[0].shape
-    for n, ref in enumerate(ins):
-        rays[n * own : (n + 1) * own] = ref[...]
+    (nz, _, edge) = outs[0].shape
+    at = 0
+    for ref in ins:
+        rays[at : at + ref.shape[0]] = ref[...]
+        at += ref.shape[0]
     acc[...] = jnp.zeros_like(acc)
 
     def body(j, t, u, p, q):
@@ -247,7 +250,7 @@
                 outs=(SMEM, VMEM),
                 work=work,
             )(*[pltpu.with_memory_space_constraint(source, pltpu.HBM) for source in sources])
-        columns = {d: along_x(column, d) for d in (RIGHT, LEFT, ACROSS)}
+        columns = {d: along_x(column, d) for d in (ACROSS, RIGHT, LEFT)}
         columns[0] = column
         mine, other = call(
             forward_kernel,
@@ -263,12 +266,12 @@
             [VMEM] * 2,
             8,
         )(mine, across(other))
-        residual, flipped = call(
-            owner_kernel, [((own, *tile), BF16)] * 2, [VMEM] * (2 + ny), 8
+        more = iteration + 1 < ITERS
+        flipped, *residual = call(
+            functools.partial(owner_kernel, ny - 1), [((own, *tile), BF16)] * (1 + (not more)), [VMEM] * (2 + ny), 8
         )(sinogram[0], weights[0], near, *[along_y(far[d - 1], d) for d in range(1, ny)])
         same = [flipped] + [along_y(flipped, d) for d in range(1, ny)]
-        rays = same + [across(value) for value in same]
-
+        rays = same + [across(same[0]), across(jnp.concatenate(same[1:]))]
         half = ((nz // 2, *tile), BF16)
         here, right_low, right_high, far_low, far_high, left_low, left_high = call(
             backward_kernel,
@@ -286,7 +289,6 @@
             here, right_low, left_low, right_high, left_high
         )
         terms = along_z(column)
-        more = iteration + 1 < ITERS
         current, *rest = call(
             functools.partial(update_kernel, step_size), [(tile, F32)] + [((nz, *tile), BF16)] * more, [VMEM] * 2, 8
         )(terms, current)
@@ -296,7 +298,7 @@
     copies = jnp.broadcast_to(image.astype(BF16)[None], (nz, *tile))
     for iteration in range(ITERS):
         current, residual, copies, table = iterate(iteration, current, copies, table)
-    return (current, residual[None])
+    return (current, residual[0][None])
 
 
 def solution(mesh):

time: 182 us -> 182 us (level)
    ppermute x10 -> x6, waiting for transfers between devices: 6.47 us -> 6.6 us  [across(): return lax.ppermute(value, 'space', [(i, i ^ 1) for i in range(n_space)])]
  transfers between devices with their start and end apart: 40 -> 36, of which waited for: 29 -> 27; matrix products, arithmetic and copies ran while one was open for 0% -> 0% of each run, Pallas kernels for 2% -> 2%
where the time goes in v4:
time: 182 us; the launch traced here: 179 us
  blocking collectives  59.2 us (33%)
  waiting for transfers between devices  54 us (30%)
  starting transfers between devices  48.8 us (27%)
  Pallas kernels  15.2 us (8%)
    all_to_all x4, blocking collectives, along_z(): lax.all_to_all(value, 'angle', 0, 0, axis_index_groups=z_groups, tiled=True)  59.2 us
    ppermute x18, starting transfers between devices, along_x(): lax.ppermute(value, 'angle', [(i, i // NX * NX + (i + d) % NX) for i in r...  27.7 us
    ppermute x18, waiting for transfers between devices, along_x(): lax.ppermute(value, 'angle', [(i, i // NX * NX + (i + d) % NX) for i in r...  26 us
    ppermute x12, waiting for transfers between devices, along_y(): lax.ppermute(value, 'space', [(i, (i + d * CORES) % n_space) for i in ran...  21.4 us
    ppermute x12, starting transfers between devices, along_y(): lax.ppermute(value, 'space', [(i, (i + d * CORES) % n_space) for i in ran...  19.8 us
    ppermute x6, waiting for transfers between devices, across(): return lax.ppermute(value, 'space', [(i, i ^ 1) for i in range(n_space)])  6.6 us
    pallas_call x2, Pallas kernels, iterate(): call(forward_kernel, [((ny * own, *tile), BF16)] * 2, [SMEM] + [VMEM] * (...  4.49 us
    pallas_call x2, Pallas kernels, iterate(): call(backward_kernel, [((nz, *tile), BF16)] + [half] * (2 * NX - 2), [SME...  4.43 us
  transfers between devices with their start and end apart: 36, of which 27 were waited for; matrix products, arithmetic and copies ran while one was open for 0% of the time, Pallas kernels for 2%

profile of v4, /device:TPU:8, one launch (start us, length us, event | category | flops | bytes accessed | tf_op | source)
XLA Modules:
  0.0 179.0 jit_solution(13272489427274678829)
XLA Ops:
  1.5 20.1 %all_to_all.20.refs_0_ = bf16[8,128,128]{2,1,0:T(8,128)(2,1)S(1)} all-to-all(bf16[8,128,128]{2,1,0:T(8,128)(2,1)S(1)} %broadcast_in_dim.4), channel_id=1, replica_groups={{0,4,8,12,16,20,24,28},{1,5,9,13,17,21,25,29},{2,6,10,14,18,22,26,30},{..., dimensions={0} | all-to-all | bytes 524288 | tf_op jit(solution)/shard_map/all_to_all | solution.py:237
  21.7 2.8 %collective-permute-start.2 = (bf16[8,128,128]{2,1,0:T(8,128)(2,1)S(1)}, bf16[8,128,128]{2,1,0:T(8,128)(2,1)S(1)}, u32[]{:S(2)}, u32[]{:S(2)}) collective-permute-start(bf16[8,128,128]{2,1,0:T(8,128)(2,1)S(1)} %all_to_all.20.refs_0_), channel_id=1, source_target_pairs={{0,3},{1,0},{2,1},{3,2},{4,7},{5,4},{6,5},{7,6},{8,11},{9,8},{10,9... | collective-permute-start | bytes 786440 | tf_op jit(solution)/shard_map/ppermute | solution.py:228
  26.1 3.9 %shard_map.86 = (s32[384]{0:T(512)S(1)}, bf16[97,128,128]{2,1,0:T(8,128)(2,1)S(1)}) custom-call(s32[96]{0:T(128)} %bitcast.12, s32[96]{0:T(128)} %bitcast.13, s32[8]{0:T(128)} %bitcast.14, bf16[96,128,128]{2,1,0:T(8,128)(2,1)} %bitcast.11), custom_call_target="tpu_custom_call" | custom-call | flops 402653184 | bytes 2097152 | tf_op jit(solution)/shard_map/pallas_call | solution.py:243
  30.1 3.9 %collective-permute-done.2.refs_3_ = bf16[8,128,128]{2,1,0:T(8,128)(2,1)S(1)} collective-permute-done((bf16[8,128,128]{2,1,0:T(8,128)(2,1)S(1)}, bf16[8,128,128]{2,1,0:T(8,128)(2,1)S(1)}, u32[]{:S(2)}, u32[]{:S(2)}) %collective-permute-start.2) | collective-permute-done | bytes 262176 | tf_op jit(solution)/shard_map/ppermute | solution.py:228
  34.9 2.8 %collective-permute-done.refs_1_ = bf16[8,128,128]{2,1,0:T(8,128)(2,1)S(1)} collective-permute-done((bf16[8,128,128]{2,1,0:T(8,128)(2,1)S(1)}, bf16[8,128,128]{2,1,0:T(8,128)(2,1)S(1)}, u32[]{:S(2)}, u32[]{:S(2)}) %collective-permute-start) | collective-permute-done | bytes 262176 | tf_op jit(solution)/shard_map/ppermute | solution.py:228
  37.6 2.2 %shard_map.87 = (bf16[16,128,128]{2,1,0:T(8,128)(2,1)S(1)}, bf16[16,128,128]{2,1,0:T(8,128)(2,1)S(1)}) custom-call(s32[384]{0:T(512)S(1)} %get-tuple-element.38.tab, bf16[97,128,128]{2,1,0:T(8,128)(2,1)S(1)} %get-tuple-element.39.tiles_ref, bf16[8,128,128]{2,1,0:T(8,128)(2,1)S(1)} %all_to_all.20.refs_0_, ...), custom_call_target="tpu_custom_call" | custom-call | flops 402653184 | bytes 2097152 | tf_op jit(solution)/shard_map/pallas_call | solution.py:255
  44.6 2.4 %collective-permute-start.6 = (bf16[4,128,128]{2,1,0:T(8,128)(2,1)S(1)}, bf16[4,128,128]{2,1,0:T(8,128)(2,1)S(1)}, u32[]{:S(2)}, u32[]{:S(2)}) collective-permute-start(bf16[4,128,128]{2,1,0:T(8,128)(2,1)S(1)} %get-tuple-element.45), channel_id=1, source_target_pairs={{0,192},{32,224},{64,0},{96,32},{128,64},{160,96},{192,128},{224,1... | collective-permute-start | bytes 393224 | tf_op jit(solution)/shard_map/ppermute | solution.py:231
  47.8 3.7 %collective-permute-done.5.refs_1_ = bf16[4,128,128]{2,1,0:T(8,128)(2,1)S(1)} collective-permute-done((bf16[4,128,128]{2,1,0:T(8,128)(2,1)S(1)}, bf16[4,128,128]{2,1,0:T(8,128)(2,1)S(1)}, u32[]{:S(2)}, u32[]{:S(2)}) %collective-permute-start.5) | collective-permute-done | bytes 131104 | tf_op jit(solution)/shard_map/ppermute | solution.py:231
  53.6 2.0 %collective-permute-start.8 = (bf16[4,128,128]{2,1,0:T(8,128)(2,1)S(1)}, bf16[4,128,128]{2,1,0:T(8,128)(2,1)S(1)}, u32[]{:S(2)}, u32[]{:S(2)}) collective-permute-start(bf16[4,128,128]{2,1,0:T(8,128)(2,1)S(1)} %shard_map.89.refs_0_), channel_id=1, source_target_pairs={{0,128},{32,160},{64,192},{96,224},{128,0},{160,32},{192,64},{224,... | collective-permute-start | bytes 393224 | tf_op jit(solution)/shard_map/ppermute | solution.py:231
  57.2 2.0 %collective-permute-done.9.refs_3_ = bf16[4,128,128]{2,1,0:T(8,128)(2,1)S(1)} collective-permute-done((bf16[4,128,128]{2,1,0:T(8,128)(2,1)S(1)}, bf16[4,128,128]{2,1,0:T(8,128)(2,1)S(1)}, u32[]{:S(2)}, u32[]{:S(2)}) %collective-permute-start.9) | collective-permute-done | bytes 131104 | tf_op jit(solution)/shard_map/ppermute | solution.py:231
  64.2 2.2 %shard_map.90 = (bf16[8,128,128]{2,1,0:T(8,128)(2,1)S(1)}, bf16[4,128,128]{2,1,0:T(8,128)(2,1)S(1)}, bf16[4,128,128]{2,1,0:T(8,128)(2,1)S(1)}, bf16[4,128,128]{2...) custom-call(s32[384]{0:T(512)S(1)} %get-tuple-element.38.tab, ...), custom_call_target="tpu_custom_call" | custom-call | flops 402653184 | bytes 2097152 | tf_op jit(solution)/shard_map/pallas_call | solution.py:276
  66.5 3.2 %collective-permute-start.13 = (bf16[4,128,128]{2,1,0:T(8,128)(2,1)S(1)}, bf16[4,128,128]{2,1,0:T(8,128)(2,1)S(1)}, u32[]{:S(2)}, u32[]{:S(2)}) collective-permute-start(bf16[4,128,128]{2,1,0:T(8,128)(2,1)S(1)} %get-tuple-element.50), channel_id=1, source_target_pairs={{0,3},{1,0},{2,1},{3,2},{4,7},{5,4},{6,5},{7,6},{8,11},{9,8},{10,9... | collective-permute-start | bytes 393224 | tf_op jit(solution)/shard_map/ppermute | solution.py:228
  69.8 2.0 %collective-permute-start.16 = (bf16[4,128,128]{2,1,0:T(8,128)(2,1)S(1)}, bf16[4,128,128]{2,1,0:T(8,128)(2,1)S(1)}, u32[]{:S(2)}, u32[]{:S(2)}) collective-permute-start(bf16[4,128,128]{2,1,0:T(8,128)(2,1)S(1)} %get-tuple-element.53), channel_id=1, source_target_pairs={{0,1},{1,2},{2,3},{3,0},{4,5},{5,6},{6,7},{7,4},{8,9},{9,10},{10,1... | collective-permute-start | bytes 393224 | tf_op jit(solution)/shard_map/ppermute | solution.py:228
  73.8 3.8 %collective-permute-start.17 = (bf16[4,128,128]{2,1,0:T(8,128)(2,1)S(1)}, bf16[4,128,128]{2,1,0:T(8,128)(2,1)S(1)}, u32[]{:S(2)}, u32[]{:S(2)}) collective-permute-start(bf16[4,128,128]{2,1,0:T(8,128)(2,1)S(1)} %get-tuple-element.54), channel_id=1, source_target_pairs={{0,3},{1,0},{2,1},{3,2},{4,7},{5,4},{6,5},{7,6},{8,11},{9,8},{10,9... | collective-permute-start | bytes 393224 | tf_op jit(solution)/shard_map/ppermute | solution.py:228
  77.6 2.9 %collective-permute-done.14.refs_0_ = bf16[4,128,128]{2,1,0:T(8,128)(2,1)S(1)} collective-permute-done((bf16[4,128,128]{2,1,0:T(8,128)(2,1)S(1)}, bf16[4,128,128]{2,1,0:T(8,128)(2,1)S(1)}, u32[]{:S(2)}, u32[]{:S(2)}) %collective-permute-start.14) | collective-permute-done | bytes 131104 | tf_op jit(solution)/shard_map/ppermute | solution.py:228
  80.5 13.3 %all_to_all.21.grad_ref = bf16[8,128,128]{2,1,0:T(8,128)(2,1)S(1)} all-to-all(bf16[8,128,128]{2,1,0:T(8,128)(2,1)S(1)} %shard_map.92), channel_id=1, replica_groups={{0,4,8,12,16,20,24,28},{1,5,9,13,17,21,25,29},{2,6,10,14,18,22,26,30},{..., dimensions={0} | all-to-all | bytes 524288 | tf_op jit(solution)/shard_map/all_to_all | solution.py:237
  93.9 12.9 %all_to_all.22.refs_0_ = bf16[8,128,128]{2,1,0:T(8,128)(2,1)S(1)} all-to-all(bf16[8,128,128]{2,1,0:T(8,128)(2,1)S(1)} %get-tuple-element.55), channel_id=1, replica_groups={{0,4,8,12,16,20,24,28},{1,5,9,13,17,21,25,29},{2,6,10,14,18,22,26,30},{..., dimensions={0} | all-to-all | bytes 524288 | tf_op jit(solution)/shard_map/all_to_all | solution.py:237
  106.8 3.3 %collective-permute-start.20 = (bf16[8,128,128]{2,1,0:T(8,128)(2,1)S(1)}, bf16[8,128,128]{2,1,0:T(8,128)(2,1)S(1)}, u32[]{:S(2)}, u32[]{:S(2)}) collective-permute-start(bf16[8,128,128]{2,1,0:T(8,128)(2,1)S(1)} %all_to_all.22.refs_0_), channel_id=1, source_target_pairs={{0,3},{1,0},{2,1},{3,2},{4,7},{5,4},{6,5},{7,6},{8,11},{9,8},{10,9... | collective-permute-start | bytes 786440 | tf_op jit(solution)/shard_map/ppermute | solution.py:228
  111.7 5.1 %collective-permute-done.20.refs_3_ = bf16[8,128,128]{2,1,0:T(8,128)(2,1)S(1)} collective-permute-done((bf16[8,128,128]{2,1,0:T(8,128)(2,1)S(1)}, bf16[8,128,128]{2,1,0:T(8,128)(2,1)S(1)}, u32[]{:S(2)}, u32[]{:S(2)}) %collective-permute-start.20) | collective-permute-done | bytes 262176 | tf_op jit(solution)/shard_map/ppermute | solution.py:228
  118.1 2.6 %collective-permute-done.18.refs_1_ = bf16[8,128,128]{2,1,0:T(8,128)(2,1)S(1)} collective-permute-done((bf16[8,128,128]{2,1,0:T(8,128)(2,1)S(1)}, bf16[8,128,128]{2,1,0:T(8,128)(2,1)S(1)}, u32[]{:S(2)}, u32[]{:S(2)}) %collective-permute-start.18) | collective-permute-done | bytes 262176 | tf_op jit(solution)/shard_map/ppermute | solution.py:228
  120.7 2.2 %shard_map.94 = (bf16[16,128,128]{2,1,0:T(8,128)(2,1)S(1)}, bf16[16,128,128]{2,1,0:T(8,128)(2,1)S(1)}) custom-call(s32[384]{0:T(512)S(1)} %get-tuple-element.38.tab, bf16[97,128,128]{2,1,0:T(8,128)(2,1)S(1)} %get-tuple-element.39.tiles_ref, bf16[8,128,128]{2,1,0:T(8,128)(2,1)S(1)} %all_to_all.22.refs_0_, ...), custom_call_target="tpu_custom_call" | custom-call | flops 402653184 | bytes 2097152 | tf_op jit(solution)/shard_map/pallas_call | solution.py:255
  126.6 3.1 %collective-permute-start.23 = (bf16[4,128,128]{2,1,0:T(8,128)(2,1)S(1)}, bf16[4,128,128]{2,1,0:T(8,128)(2,1)S(1)}, u32[]{:S(2)}, u32[]{:S(2)}) collective-permute-start(bf16[4,128,128]{2,1,0:T(8,128)(2,1)S(1)} %get-tuple-element.60), channel_id=1, source_target_pairs={{0,128},{32,160},{64,192},{96,224},{128,0},{160,32},{192,64},{224,... | collective-permute-start | bytes 393224 | tf_op jit(solution)/shard_map/ppermute | solution.py:231
  129.7 2.3 %collective-permute-done.22.refs_0_ = bf16[4,128,128]{2,1,0:T(8,128)(2,1)S(1)} collective-permute-done((bf16[4,128,128]{2,1,0:T(8,128)(2,1)S(1)}, bf16[4,128,128]{2,1,0:T(8,128)(2,1)S(1)}, u32[]{:S(2)}, u32[]{:S(2)}) %collective-permute-start.22) | collective-permute-done | bytes 131104 | tf_op jit(solution)/shard_map/ppermute | solution.py:231
  132.0 2.4 %collective-permute-done.23.refs_1_ = bf16[4,128,128]{2,1,0:T(8,128)(2,1)S(1)} collective-permute-done((bf16[4,128,128]{2,1,0:T(8,128)(2,1)S(1)}, bf16[4,128,128]{2,1,0:T(8,128)(2,1)S(1)}, u32[]{:S(2)}, u32[]{:S(2)}) %collective-permute-start.23) | collective-permute-done | bytes 131104 | tf_op jit(solution)/shard_map/ppermute | solution.py:231
  139.8 2.6 %collective-permute-start.25 = (bf16[4,128,128]{2,1,0:T(8,128)(2,1)S(1)}, bf16[4,128,128]{2,1,0:T(8,128)(2,1)S(1)}, u32[]{:S(2)}, u32[]{:S(2)}) collective-permute-start(bf16[4,128,128]{2,1,0:T(8,128)(2,1)S(1)} %get-tuple-element.62.refs_0_), channel_id=1, source_target_pairs={{0,64},{32,96},{64,128},{96,160},{128,192},{160,224},{192,0},{224,... | collective-permute-start | bytes 393224 | tf_op jit(solution)/shard_map/ppermute | solution.py:231
  142.5 3.7 %collective-permute-done.26.refs_2_ = bf16[4,128,128]{2,1,0:T(8,128)(2,1)S(1)} collective-permute-done((bf16[4,128,128]{2,1,0:T(8,128)(2,1)S(1)}, bf16[4,128,128]{2,1,0:T(8,128)(2,1)S(1)}, u32[]{:S(2)}, u32[]{:S(2)}) %collective-permute-start.26) | collective-permute-done | bytes 131104 | tf_op jit(solution)/shard_map/ppermute | solution.py:231
  149.1 2.2 %shard_map.97 = (bf16[8,128,128]{2,1,0:T(8,128)(2,1)S(1)}, bf16[4,128,128]{2,1,0:T(8,128)(2,1)S(1)}, bf16[4,128,128]{2,1,0:T(8,128)(2,1)S(1)}, bf16[4,128,128]{2...) custom-call(s32[384]{0:T(512)S(1)} %get-tuple-element.38.tab, ...), custom_call_target="tpu_custom_call" | custom-call | flops 402653184 | bytes 2097152 | tf_op jit(solution)/shard_map/pallas_call | solution.py:276
  151.4 3.2 %collective-permute-start.31 = (bf16[4,128,128]{2,1,0:T(8,128)(2,1)S(1)}, bf16[4,128,128]{2,1,0:T(8,128)(2,1)S(1)}, u32[]{:S(2)}, u32[]{:S(2)}) collective-permute-start(bf16[4,128,128]{2,1,0:T(8,128)(2,1)S(1)} %get-tuple-element.67), channel_id=1, source_target_pairs={{0,3},{1,0},{2,1},{3,2},{4,7},{5,4},{6,5},{7,6},{8,11},{9,8},{10,9... | collective-permute-start | bytes 393224 | tf_op jit(solution)/shard_map/ppermute | solution.py:228
  154.6 2.0 %collective-permute-start.34 = (bf16[4,128,128]{2,1,0:T(8,128)(2,1)S(1)}, bf16[4,128,128]{2,1,0:T(8,128)(2,1)S(1)}, u32[]{:S(2)}, u32[]{:S(2)}) collective-permute-start(bf16[4,128,128]{2,1,0:T(8,128)(2,1)S(1)} %get-tuple-element.70), channel_id=1, source_target_pairs={{0,1},{1,2},{2,3},{3,0},{4,5},{5,6},{6,7},{7,4},{8,9},{9,10},{10,1... | collective-permute-start | bytes 393224 | tf_op jit(solution)/shard_map/ppermute | solution.py:228
  158.7 3.8 %collective-permute-start.35 = (bf16[4,128,128]{2,1,0:T(8,128)(2,1)S(1)}, bf16[4,128,128]{2,1,0:T(8,128)(2,1)S(1)}, u32[]{:S(2)}, u32[]{:S(2)}) collective-permute-start(bf16[4,128,128]{2,1,0:T(8,128)(2,1)S(1)} %get-tuple-element.71), channel_id=1, source_target_pairs={{0,3},{1,0},{2,1},{3,2},{4,7},{5,4},{6,5},{7,6},{8,11},{9,8},{10,9... | collective-permute-start | bytes 393224 | tf_op jit(solution)/shard_map/ppermute | solution.py:228
  162.4 2.9 %collective-permute-done.32.refs_0_ = bf16[4,128,128]{2,1,0:T(8,128)(2,1)S(1)} collective-permute-done((bf16[4,128,128]{2,1,0:T(8,128)(2,1)S(1)}, bf16[4,128,128]{2,1,0:T(8,128)(2,1)S(1)}, u32[]{:S(2)}, u32[]{:S(2)}) %collective-permute-start.32) | collective-permute-done | bytes 131104 | tf_op jit(solution)/shard_map/ppermute | solution.py:228
  165.4 12.9 %all_to_all.23.grad_ref = bf16[8,128,128]{2,1,0:T(8,128)(2,1)S(1)} all-to-all(bf16[8,128,128]{2,1,0:T(8,128)(2,1)S(1)} %shard_map.99), channel_id=1, replica_groups={{0,4,8,12,16,20,24,28},{1,5,9,13,17,21,25,29},{2,6,10,14,18,22,26,30},{..., dimensions={0} | all-to-all | bytes 524288 | tf_op jit(solution)/shard_map/all_to_all | solution.py:237
  (69 shorter events, 37.8 us)
Async XLA Ops:
  21.7 12.3 %collective-permute-start.2 = (bf16[8,128,128]{2,1,0:T(8,128)(2,1)S(1)}, bf16[8,128,128]{2,1,0:T(8,128)(2,1)S(1)}, u32[]{:S(2)}, u32[]{:S(2)}) collective-permute-start(bf16[8,128,128]{2,1,0:T(8,128)(2,1)S(1)} %all_to_all.20.refs_0_), channel_id=1, source_target_pairs={{0,3},{1,0},{2,1},{3,2},{4,7},{5,4},{6,5},{7,6},{8,11},{9,8},{10,9... | collective-permute-start | bytes 786440 | tf_op jit(solution)/shard_map/ppermute | solution.py:228
  24.4 10.5 %collective-permute-start.1 = (bf16[8,128,128]{2,1,0:T(8,128)(2,1)S(1)}, bf16[8,128,128]{2,1,0:T(8,128)(2,1)S(1)}, u32[]{:S(2)}, u32[]{:S(2)}) collective-permute-start(bf16[8,128,128]{2,1,0:T(8,128)(2,1)S(1)} %all_to_all.20.refs_0_), channel_id=1, source_target_pairs={{0,2},{1,3},{2,0},{3,1},{4,6},{5,7},{6,4},{7,5},{8,10},{9,11},{10,... | collective-permute-start | bytes 786440 | tf_op jit(solution)/shard_map/ppermute | solution.py:228
  25.2 12.4 %collective-permute-start = (bf16[8,128,128]{2,1,0:T(8,128)(2,1)S(1)}, bf16[8,128,128]{2,1,0:T(8,128)(2,1)S(1)}, u32[]{:S(2)}, u32[]{:S(2)}) collective-permute-start(bf16[8,128,128]{2,1,0:T(8,128)(2,1)S(1)} %all_to_all.20.refs_0_), channel_id=1, source_target_pairs={{0,1},{1,2},{2,3},{3,0},{4,5},{5,6},{6,7},{7,4},{8,9},{9,10},{10,1... | collective-permute-start | bytes 786440 | tf_op jit(solution)/shard_map/ppermute | solution.py:228
  42.0 5.8 %collective-permute-start.4 = (bf16[4,128,128]{2,1,0:T(8,128)(2,1)S(1)}, bf16[4,128,128]{2,1,0:T(8,128)(2,1)S(1)}, u32[]{:S(2)}, u32[]{:S(2)}) collective-permute-start(bf16[4,128,128]{2,1,0:T(8,128)(2,1)S(1)} %get-tuple-element.43), channel_id=1, source_target_pairs={{0,64},{32,96},{64,128},{96,160},{128,192},{160,224},{192,0},{224,... | collective-permute-start | bytes 393224 | tf_op jit(solution)/shard_map/ppermute | solution.py:231
  43.7 7.9 %collective-permute-start.5 = (bf16[4,128,128]{2,1,0:T(8,128)(2,1)S(1)}, bf16[4,128,128]{2,1,0:T(8,128)(2,1)S(1)}, u32[]{:S(2)}, u32[]{:S(2)}) collective-permute-start(bf16[4,128,128]{2,1,0:T(8,128)(2,1)S(1)} %get-tuple-element.44), channel_id=1, source_target_pairs={{0,128},{32,160},{64,192},{96,224},{128,0},{160,32},{192,64},{224,... | collective-permute-start | bytes 393224 | tf_op jit(solution)/shard_map/ppermute | solution.py:231
  44.6 7.9 %collective-permute-start.6 = (bf16[4,128,128]{2,1,0:T(8,128)(2,1)S(1)}, bf16[4,128,128]{2,1,0:T(8,128)(2,1)S(1)}, u32[]{:S(2)}, u32[]{:S(2)}) collective-permute-start(bf16[4,128,128]{2,1,0:T(8,128)(2,1)S(1)} %get-tuple-element.45), channel_id=1, source_target_pairs={{0,192},{32,224},{64,0},{96,32},{128,64},{160,96},{192,128},{224,1... | collective-permute-start | bytes 393224 | tf_op jit(solution)/shard_map/ppermute | solution.py:231
  52.7 6.4 %collective-permute-start.9 = (bf16[4,128,128]{2,1,0:T(8,128)(2,1)S(1)}, bf16[4,128,128]{2,1,0:T(8,128)(2,1)S(1)}, u32[]{:S(2)}, u32[]{:S(2)}) collective-permute-start(bf16[4,128,128]{2,1,0:T(8,128)(2,1)S(1)} %shard_map.89.refs_0_), channel_id=1, source_target_pairs={{0,192},{32,224},{64,0},{96,32},{128,64},{160,96},{192,128},{224,1... | collective-permute-start | bytes 393224 | tf_op jit(solution)/shard_map/ppermute | solution.py:231
  53.6 7.3 %collective-permute-start.8 = (bf16[4,128,128]{2,1,0:T(8,128)(2,1)S(1)}, bf16[4,128,128]{2,1,0:T(8,128)(2,1)S(1)}, u32[]{:S(2)}, u32[]{:S(2)}) collective-permute-start(bf16[4,128,128]{2,1,0:T(8,128)(2,1)S(1)} %shard_map.89.refs_0_), channel_id=1, source_target_pairs={{0,128},{32,160},{64,192},{96,224},{128,0},{160,32},{192,64},{224,... | collective-permute-start | bytes 393224 | tf_op jit(solution)/shard_map/ppermute | solution.py:231
  55.6 6.6 %collective-permute-start.7 = (bf16[4,128,128]{2,1,0:T(8,128)(2,1)S(1)}, bf16[4,128,128]{2,1,0:T(8,128)(2,1)S(1)}, u32[]{:S(2)}, u32[]{:S(2)}) collective-permute-start(bf16[4,128,128]{2,1,0:T(8,128)(2,1)S(1)} %shard_map.89.refs_0_), channel_id=1, source_target_pairs={{0,64},{32,96},{64,128},{96,160},{128,192},{160,224},{192,0},{224,... | collective-permute-start | bytes 393224 | tf_op jit(solution)/shard_map/ppermute | solution.py:231
  62.2 2.0 %collective-permute-start.11 = (bf16[12,128,128]{2,1,0:T(8,128)(2,1)S(1)}, bf16[12,128,128]{2,1,0:T(8,128)(2,1)S(1)}, u32[]{:S(2)}, u32[]{:S(2)}) collective-permute-start(bf16[12,128,128]{2,1,0:T(8,128)(2,1)S(1)} %pad_maximum_fusion), channel_id=1, source_target_pairs={{0,32},{32,0},{64,96},{96,64},{128,160},{160,128},{192,224},{224,1... | collective-permute-start | bytes 1179656 | tf_op jit(solution)/shard_map/ppermute | solution.py:234
  66.4 6.9 %collective-permute-start.12 = (bf16[4,128,128]{2,1,0:T(8,128)(2,1)S(1)}, bf16[4,128,128]{2,1,0:T(8,128)(2,1)S(1)}, u32[]{:S(2)}, u32[]{:S(2)}) collective-permute-start(bf16[4,128,128]{2,1,0:T(8,128)(2,1)S(1)} %get-tuple-element.48), channel_id=1, source_target_pairs={{0,1},{1,2},{2,3},{3,0},{4,5},{5,6},{6,7},{7,4},{8,9},{9,10},{10,1... | collective-permute-start | bytes 393224 | tf_op jit(solution)/shard_map/ppermute | solution.py:228
  66.5 7.1 %collective-permute-start.13 = (bf16[4,128,128]{2,1,0:T(8,128)(2,1)S(1)}, bf16[4,128,128]{2,1,0:T(8,128)(2,1)S(1)}, u32[]{:S(2)}, u32[]{:S(2)}) collective-permute-start(bf16[4,128,128]{2,1,0:T(8,128)(2,1)S(1)} %get-tuple-element.50), channel_id=1, source_target_pairs={{0,3},{1,0},{2,1},{3,2},{4,7},{5,4},{6,5},{7,6},{8,11},{9,8},{10,9... | collective-permute-start | bytes 393224 | tf_op jit(solution)/shard_map/ppermute | solution.py:228
  69.7 7.8 %collective-permute-start.15 = (bf16[4,128,128]{2,1,0:T(8,128)(2,1)S(1)}, bf16[4,128,128]{2,1,0:T(8,128)(2,1)S(1)}, u32[]{:S(2)}, u32[]{:S(2)}) collective-permute-start(bf16[4,128,128]{2,1,0:T(8,128)(2,1)S(1)} %get-tuple-element.52), channel_id=1, source_target_pairs={{0,3},{1,0},{2,1},{3,2},{4,7},{5,4},{6,5},{7,6},{8,11},{9,8},{10,9... | collective-permute-start | bytes 393224 | tf_op jit(solution)/shard_map/ppermute | solution.py:228
  69.8 7.8 %collective-permute-start.16 = (bf16[4,128,128]{2,1,0:T(8,128)(2,1)S(1)}, bf16[4,128,128]{2,1,0:T(8,128)(2,1)S(1)}, u32[]{:S(2)}, u32[]{:S(2)}) collective-permute-start(bf16[4,128,128]{2,1,0:T(8,128)(2,1)S(1)} %get-tuple-element.53), channel_id=1, source_target_pairs={{0,1},{1,2},{2,3},{3,0},{4,5},{5,6},{6,7},{7,4},{8,9},{9,10},{10,1... | collective-permute-start | bytes 393224 | tf_op jit(solution)/shard_map/ppermute | solution.py:228
  73.7 6.7 %collective-permute-start.14 = (bf16[4,128,128]{2,1,0:T(8,128)(2,1)S(1)}, bf16[4,128,128]{2,1,0:T(8,128)(2,1)S(1)}, u32[]{:S(2)}, u32[]{:S(2)}) collective-permute-start(bf16[4,128,128]{2,1,0:T(8,128)(2,1)S(1)} %get-tuple-element.51), channel_id=1, source_target_pairs={{0,1},{1,2},{2,3},{3,0},{4,5},{5,6},{6,7},{7,4},{8,9},{9,10},{10,1... | collective-permute-start | bytes 393224 | tf_op jit(solution)/shard_map/ppermute | solution.py:228
  73.8 6.6 %collective-permute-start.17 = (bf16[4,128,128]{2,1,0:T(8,128)(2,1)S(1)}, bf16[4,128,128]{2,1,0:T(8,128)(2,1)S(1)}, u32[]{:S(2)}, u32[]{:S(2)}) collective-permute-start(bf16[4,128,128]{2,1,0:T(8,128)(2,1)S(1)} %get-tuple-element.54), channel_id=1, source_target_pairs={{0,3},{1,0},{2,1},{3,2},{4,7},{5,4},{6,5},{7,6},{8,11},{9,8},{10,9... | collective-permute-start | bytes 393224 | tf_op jit(solution)/shard_map/ppermute | solution.py:228
  106.8 10.0 %collective-permute-start.20 = (bf16[8,128,128]{2,1,0:T(8,128)(2,1)S(1)}, bf16[8,128,128]{2,1,0:T(8,128)(2,1)S(1)}, u32[]{:S(2)}, u32[]{:S(2)}) collective-permute-start(bf16[8,128,128]{2,1,0:T(8,128)(2,1)S(1)} %all_to_all.22.refs_0_), channel_id=1, source_target_pairs={{0,3},{1,0},{2,1},{3,2},{4,7},{5,4},{6,5},{7,6},{8,11},{9,8},{10,9... | collective-permute-start | bytes 786440 | tf_op jit(solution)/shard_map/ppermute | solution.py:228
  110.1 8.0 %collective-permute-start.19 = (bf16[8,128,128]{2,1,0:T(8,128)(2,1)S(1)}, bf16[8,128,128]{2,1,0:T(8,128)(2,1)S(1)}, u32[]{:S(2)}, u32[]{:S(2)}) collective-permute-start(bf16[8,128,128]{2,1,0:T(8,128)(2,1)S(1)} %all_to_all.22.refs_0_), channel_id=1, source_target_pairs={{0,2},{1,3},{2,0},{3,1},{4,6},{5,7},{6,4},{7,5},{8,10},{9,11},{10,... | collective-permute-start | bytes 786440 | tf_op jit(solution)/shard_map/ppermute | solution.py:228
  110.3 10.4 %collective-permute-start.18 = (bf16[8,128,128]{2,1,0:T(8,128)(2,1)S(1)}, bf16[8,128,128]{2,1,0:T(8,128)(2,1)S(1)}, u32[]{:S(2)}, u32[]{:S(2)}) collective-permute-start(bf16[8,128,128]{2,1,0:T(8,128)(2,1)S(1)} %all_to_all.22.refs_0_), channel_id=1, source_target_pairs={{0,1},{1,2},{2,3},{3,0},{4,5},{5,6},{6,7},{7,4},{8,9},{9,10},{10,1... | collective-permute-start | bytes 786440 | tf_op jit(solution)/shard_map/ppermute | solution.py:228
  125.0 7.0 %collective-permute-start.22 = (bf16[4,128,128]{2,1,0:T(8,128)(2,1)S(1)}, bf16[4,128,128]{2,1,0:T(8,128)(2,1)S(1)}, u32[]{:S(2)}, u32[]{:S(2)}) collective-permute-start(bf16[4,128,128]{2,1,0:T(8,128)(2,1)S(1)} %get-tuple-element.59), channel_id=1, source_target_pairs={{0,64},{32,96},{64,128},{96,160},{128,192},{160,224},{192,0},{224,... | collective-permute-start | bytes 393224 | tf_op jit(solution)/shard_map/ppermute | solution.py:231
  126.6 7.9 %collective-permute-start.23 = (bf16[4,128,128]{2,1,0:T(8,128)(2,1)S(1)}, bf16[4,128,128]{2,1,0:T(8,128)(2,1)S(1)}, u32[]{:S(2)}, u32[]{:S(2)}) collective-permute-start(bf16[4,128,128]{2,1,0:T(8,128)(2,1)S(1)} %get-tuple-element.60), channel_id=1, source_target_pairs={{0,128},{32,160},{64,192},{96,224},{128,0},{160,32},{192,64},{224,... | collective-permute-start | bytes 393224 | tf_op jit(solution)/shard_map/ppermute | solution.py:231
  129.7 6.4 %collective-permute-start.24 = (bf16[4,128,128]{2,1,0:T(8,128)(2,1)S(1)}, bf16[4,128,128]{2,1,0:T(8,128)(2,1)S(1)}, u32[]{:S(2)}, u32[]{:S(2)}) collective-permute-start(bf16[4,128,128]{2,1,0:T(8,128)(2,1)S(1)} %get-tuple-element.61), channel_id=1, source_target_pairs={{0,192},{32,224},{64,0},{96,32},{128,64},{160,96},{192,128},{224,1... | collective-permute-start | bytes 393224 | tf_op jit(solution)/shard_map/ppermute | solution.py:231
  136.9 5.6 %collective-permute-start.27 = (bf16[4,128,128]{2,1,0:T(8,128)(2,1)S(1)}, bf16[4,128,128]{2,1,0:T(8,128)(2,1)S(1)}, u32[]{:S(2)}, u32[]{:S(2)}) collective-permute-start(bf16[4,128,128]{2,1,0:T(8,128)(2,1)S(1)} %get-tuple-element.62.refs_0_), channel_id=1, source_target_pairs={{0,192},{32,224},{64,0},{96,32},{128,64},{160,96},{192,128},{224,1... | collective-permute-start | bytes 393224 | tf_op jit(solution)/shard_map/ppermute | solution.py:231
  138.6 7.5 %collective-permute-start.26 = (bf16[4,128,128]{2,1,0:T(8,128)(2,1)S(1)}, bf16[4,128,128]{2,1,0:T(8,128)(2,1)S(1)}, u32[]{:S(2)}, u32[]{:S(2)}) collective-permute-start(bf16[4,128,128]{2,1,0:T(8,128)(2,1)S(1)} %get-tuple-element.62.refs_0_), channel_id=1, source_target_pairs={{0,128},{32,160},{64,192},{96,224},{128,0},{160,32},{192,64},{224,... | collective-permute-start | bytes 393224 | tf_op jit(solution)/shard_map/ppermute | solution.py:231
  139.8 7.2 %collective-permute-start.25 = (bf16[4,128,128]{2,1,0:T(8,128)(2,1)S(1)}, bf16[4,128,128]{2,1,0:T(8,128)(2,1)S(1)}, u32[]{:S(2)}, u32[]{:S(2)}) collective-permute-start(bf16[4,128,128]{2,1,0:T(8,128)(2,1)S(1)} %get-tuple-element.62.refs_0_), channel_id=1, source_target_pairs={{0,64},{32,96},{64,128},{96,160},{128,192},{160,224},{192,0},{224,... | collective-permute-start | bytes 393224 | tf_op jit(solution)/shard_map/ppermute | solution.py:231
  147.1 2.0 %collective-permute-start.29 = (bf16[12,128,128]{2,1,0:T(8,128)(2,1)S(1)}, bf16[12,128,128]{2,1,0:T(8,128)(2,1)S(1)}, u32[]{:S(2)}, u32[]{:S(2)}) collective-permute-start(bf16[12,128,128]{2,1,0:T(8,128)(2,1)S(1)} %pad_maximum_fusion.1), channel_id=1, source_target_pairs={{0,32},{32,0},{64,96},{96,64},{128,160},{160,128},{192,224},{224,1... | collective-permute-start | bytes 1179656 | tf_op jit(solution)/shard_map/ppermute | solution.py:234
  151.3 6.9 %collective-permute-start.30 = (bf16[4,128,128]{2,1,0:T(8,128)(2,1)S(1)}, bf16[4,128,128]{2,1,0:T(8,128)(2,1)S(1)}, u32[]{:S(2)}, u32[]{:S(2)}) collective-permute-start(bf16[4,128,128]{2,1,0:T(8,128)(2,1)S(1)} %get-tuple-element.65), channel_id=1, source_target_pairs={{0,1},{1,2},{2,3},{3,0},{4,5},{5,6},{6,7},{7,4},{8,9},{9,10},{10,1... | collective-permute-start | bytes 393224 | tf_op jit(solution)/shard_map/ppermute | solution.py:228
  151.4 7.1 %collective-permute-start.31 = (bf16[4,128,128]{2,1,0:T(8,128)(2,1)S(1)}, bf16[4,128,128]{2,1,0:T(8,128)(2,1)S(1)}, u32[]{:S(2)}, u32[]{:S(2)}) collective-permute-start(bf16[4,128,128]{2,1,0:T(8,128)(2,1)S(1)} %get-tuple-element.67), channel_id=1, source_target_pairs={{0,3},{1,0},{2,1},{3,2},{4,7},{5,4},{6,5},{7,6},{8,11},{9,8},{10,9... | collective-permute-start | bytes 393224 | tf_op jit(solution)/shard_map/ppermute | solution.py:228
  154.6 7.8 %collective-permute-start.33 = (bf16[4,128,128]{2,1,0:T(8,128)(2,1)S(1)}, bf16[4,128,128]{2,1,0:T(8,128)(2,1)S(1)}, u32[]{:S(2)}, u32[]{:S(2)}) collective-permute-start(bf16[4,128,128]{2,1,0:T(8,128)(2,1)S(1)} %get-tuple-element.69), channel_id=1, source_target_pairs={{0,3},{1,0},{2,1},{3,2},{4,7},{5,4},{6,5},{7,6},{8,11},{9,8},{10,9... | collective-permute-start | bytes 393224 | tf_op jit(solution)/shard_map/ppermute | solution.py:228
  154.6 7.8 %collective-permute-start.34 = (bf16[4,128,128]{2,1,0:T(8,128)(2,1)S(1)}, bf16[4,128,128]{2,1,0:T(8,128)(2,1)S(1)}, u32[]{:S(2)}, u32[]{:S(2)}) collective-permute-start(bf16[4,128,128]{2,1,0:T(8,128)(2,1)S(1)} %get-tuple-element.70), channel_id=1, source_target_pairs={{0,1},{1,2},{2,3},{3,0},{4,5},{5,6},{6,7},{7,4},{8,9},{9,10},{10,1... | collective-permute-start | bytes 393224 | tf_op jit(solution)/shard_map/ppermute | solution.py:228
  158.6 6.7 %collective-permute-start.32 = (bf16[4,128,128]{2,1,0:T(8,128)(2,1)S(1)}, bf16[4,128,128]{2,1,0:T(8,128)(2,1)S(1)}, u32[]{:S(2)}, u32[]{:S(2)}) collective-permute-start(bf16[4,128,128]{2,1,0:T(8,128)(2,1)S(1)} %get-tuple-element.68), channel_id=1, source_target_pairs={{0,1},{1,2},{2,3},{3,0},{4,5},{5,6},{6,7},{7,4},{8,9},{9,10},{10,1... | collective-permute-start | bytes 393224 | tf_op jit(solution)/shard_map/ppermute | solution.py:228
  158.7 6.6 %collective-permute-start.35 = (bf16[4,128,128]{2,1,0:T(8,128)(2,1)S(1)}, bf16[4,128,128]{2,1,0:T(8,128)(2,1)S(1)}, u32[]{:S(2)}, u32[]{:S(2)}) collective-permute-start(bf16[4,128,128]{2,1,0:T(8,128)(2,1)S(1)} %get-tuple-element.71), channel_id=1, source_target_pairs={{0,3},{1,0},{2,1},{3,2},{4,7},{5,4},{6,5},{7,6},{8,11},{9,8},{10,9... | collective-permute-start | bytes 393224 | tf_op jit(solution)/shard_map/ppermute | solution.py:228
  (7 other events, 84.4 us)
